TPU v7x, 512 devices: a whole 4x4x16 slice. The times are simulated.
512 devices in a mesh: row: 16 (over x, y), col: 32 (over z, core).
Axes of the slice: x: 4, y: 4, z: 16, core: 2. Of those that a mesh axis runs over, the one named last changes fastest.
Arguments:
- l_rows: float32 [4096, 16384], P('row', 'col'), may hold values from -6 to 6
- v_prev: float32 [16384, 1024], P('col', 'row'), may hold values from -0.046875 to 0.046875
- l_tail: float32 [4096, 4096], P('row', 'col'), may hold values from -5 to 100, as said below
- k_cross: float32 [4096, 1024], P('row', 'col'), may hold values from -6 to 6
- k_query: float32 [1024, 1024], P('row', 'col'), may hold values from -2 to 5, as said below
Outputs:
- tail_solution: float32 [4096, 1024], P('row', 'col')
- posterior: float32 [1024, 1024], P('row', 'col')
Inputs may be any that keep to these rules, and one draw needn't show every extreme that they name: `l_tail`: lower triangular; its diagonal lies between 40 and 100. `k_query`: symmetric.
All inputs are finite; a program needn't handle non-finite values.
Results may differ from a plain program's by a relative error of at most 0.000076.
Values sent between devices are 32-bit elements; how exact they have to be, the bound alone decides.
No kernel may reach another device: no remote copies, remote signals or barrier semaphores. Data moves between devices by JAX's collectives and lax.ppermute only.
A program may use at most 64 MiB of HBM per device.

v0:
```python
import functools
import jax
import jax.numpy as jnp
from jax import lax
from jax.experimental import pallas as pl
from jax.experimental.pallas import tpu as pltpu
from jax.sharding import Mesh, PartitionSpec as P


HI = lax.Precision.HIGHEST
PLANE_T = ("y", "x")
GRANT = 16 * 1024 * 1024
VMEM = pl.BlockSpec(memory_space=pltpu.VMEM)


def contract(a, b, dims):
    return lax.dot_general(a, b, (dims, ((), ())), precision=HI, preferred_element_type=jnp.float32)


def mul(a, b):
    return jnp.dot(a, b, precision=HI, preferred_element_type=jnp.float32)


def share(value, axis, count):
    return lax.all_to_all(jnp.broadcast_to(value[None], (count,) + value.shape), axis, 0, 0)


def swap(value):
    return lax.ppermute(value, "k", [(0, 1), (1, 0)])


def f32(*shape):
    return jax.ShapeDtypeStruct(shape, jnp.float32)


def local(kernel, out_shape, *operands, flops=0):
    outs = out_shape if isinstance(out_shape, tuple) else (out_shape,)
    moved = sum(4 * o.size for o in operands) + sum(4 * o.size for o in outs)
    return pl.pallas_call(
        kernel,
        out_shape=out_shape,
        in_specs=[VMEM] * len(operands),
        out_specs=tuple(VMEM for _ in outs) if isinstance(out_shape, tuple) else VMEM,
        cost_estimate=pl.CostEstimate(flops=flops, bytes_accessed=moved, transcendentals=0),
        compiler_params=pltpu.CompilerParams(vmem_limit_bytes=GRANT),
    )(*operands)


def invert_kernel(own_ref, other_ref, o_ref, full):
    first = lax.axis_index("k") == 0
    a, b = own_ref[...], other_ref[...]
    u = jnp.concatenate([jnp.where(first, a, b), jnp.where(first, b, a)], axis=0)
    n = u.shape[0]
    row = lax.broadcasted_iota(jnp.int32, (n, n), 0)
    col = lax.broadcasted_iota(jnp.int32, (n, n), 1)
    x = jnp.where(row == col, 1.0 / u, 0.0)
    s = 0
    while (1 << s) < n:
        above = ((row >> (s + 1)) == (col >> (s + 1))) & (((row >> s) & 1) == 0) & (((col >> s) & 1) == 1)
        x = x - mul(mul(x, jnp.where(above, u, 0.0)), x)
        s += 1
    full[...] = x
    half = o_ref.shape[0]
    o_ref[...] = full[pl.ds(pl.multiple_of(lax.axis_index("k") * half, half), half), :]


def invert(own, other):
    half, n = own.shape
    return pl.pallas_call(
        invert_kernel,
        out_shape=f32(half, n),
        in_specs=[VMEM, VMEM],
        out_specs=VMEM,
        scratch_shapes=[pltpu.VMEM((n, n), jnp.float32)],
        cost_estimate=pl.CostEstimate(flops=32 * 6 * n * n * n, bytes_accessed=12 * half * n, transcendentals=0),
        compiler_params=pltpu.CompilerParams(vmem_limit_bytes=GRANT),
        name="invert_block",
    )(own, other)


def pack_kernel(own_ref, o_ref):
    half = o_ref.shape[1]
    rows = pl.ds(pl.multiple_of(lax.axis_index("k") * half, half), half)
    for slot, block in enumerate((lax.axis_index("y"), 0, 1)):
        o_ref[slot] = own_ref[block, rows, :]


def rows_kernel(own_ref, mine_ref, other_ref, o_ref):
    y = lax.axis_index("y")
    first = lax.axis_index("k") == 0
    n = own_ref.shape[1]

    def block(slot):
        a, b = mine_ref[slot], other_ref[slot]
        return jnp.concatenate([jnp.where(first, a, b), jnp.where(first, b, a)], axis=0)

    diag = own_ref[y]
    a = mul(own_ref[:3].reshape(3 * n, n), diag)
    zero = jnp.zeros_like(diag)
    near, far = block(0), block(3)
    y2 = jnp.where(y > 2, -mul(near, a[2 * n :]), zero)
    t1 = a[n : 2 * n] + mul(block(2), y2)
    y1 = jnp.where(y > 1, -mul(jnp.where(y > 2, far, near), t1), zero)
    t0 = a[:n] + mul(jnp.where(y > 2, block(4), block(1)), y1) + mul(block(1), y2)
    y0 = jnp.where(y > 0, -mul(jnp.where(y > 2, block(5), jnp.where(y > 1, far, near)), t0), zero)
    for m, value in enumerate((y0, y1, y2, zero)):
        o_ref[m] = jnp.where(y == m, diag, value)


def solve_kernel(j, right_ref, inv_ref, *refs):
    new_ref, sent_ref = refs[-2:]
    value = jnp.zeros(new_ref.shape, jnp.float32)
    for m in range(4):
        right = right_ref[m] if j == 0 else sum(right_ref[s, m] for s in range(4))
        value = value + mul(right, inv_ref[m])
    if j > 0:
        value = jnp.where(lax.axis_index("x") == j, value, refs[0][...])
    new_ref[...] = value
    for to in range(4):
        sent_ref[to] = value


def gram_kernel(all_ref, own_ref, o_ref):
    every = all_ref[...].reshape(-1, own_ref.shape[1])
    o_ref[...] = lax.dot_general(own_ref[...], every, (((1,), (1,)), ((), ())), precision=HI, preferred_element_type=jnp.float32)


def split_kernel(near_ref, all_ref, own_ref, o_ref):
    qc = own_ref.shape[0]
    every = all_ref[...].reshape(-1, own_ref.shape[1])
    far = lax.dot_general(own_ref[...], every, (((1,), (1,)), ((), ())), precision=HI, preferred_element_type=jnp.float32)
    near = near_ref[...]
    lane = lax.broadcasted_iota(jnp.int32, (qc, 128), 1)
    for c in range(16):
        at = c * qc // 128 * 128
        shift = c * qc % 128
        a = pltpu.roll(near[:, at : at + 128], (128 - shift) % 128, 1)
        b = pltpu.roll(far[:, at : at + 128], (128 - shift + qc) % 128, 1)
        value = jnp.where(lane < qc, a, b)
        low = pltpu.roll(value[qc // 2 :], 64, 1)
        o_ref[c] = jnp.where(lane[: qc // 2] < 2 * qc, value[: qc // 2], low)


def final_kernel(part_ref, prior_ref, query_ref, o_ref):
    total = part_ref[0]
    for s in range(1, part_ref.shape[0]):
        total = total + part_ref[s]
    total = jnp.concatenate([total, pltpu.roll(total, 64, 1)], axis=0)
    qc = total.shape[0]
    lane = lax.broadcasted_iota(jnp.int32, total.shape, 1)
    turned = jnp.where(lane < qc, pltpu.roll(total, 128 - qc, 1), pltpu.roll(total, qc, 1))
    total = jnp.where(lax.axis_index("k") == 0, total, turned)
    o_ref[...] = query_ref[...] - (prior_ref[...] + total[:, : 2 * qc])


def update_kernel(j, got_ref, panel_ref, old_ref, new_ref, sent_ref, held, sems):
    copies = [pltpu.make_async_copy(panel_ref.at[j, m], held.at[m], sems.at[m]) for m in range(4)]
    for copy in copies:
        copy.start()
    known = got_ref[j]
    for m in range(4):
        old = jnp.where(lax.axis_index("y") == m, old_ref[...], 0.0) if j == 0 else old_ref[m]
        copies[m].wait()
        value = old - mul(known, held[m])
        new_ref[m] = value
        for to in range(4):
            sent_ref[to, m] = value


def update(j, got, panels, old):
    qc, n = got.shape[1:]
    return pl.pallas_call(
        functools.partial(update_kernel, j),
        out_shape=(f32(4, qc, n), f32(4, 4, qc, n)),
        in_specs=[VMEM, pl.BlockSpec(memory_space=pltpu.HBM), VMEM],
        out_specs=(VMEM, VMEM),
        scratch_shapes=[pltpu.VMEM((4, n, n), jnp.float32), pltpu.SemaphoreType.DMA((4,))],
        cost_estimate=pl.CostEstimate(flops=12 * 4 * qc * n * n, bytes_accessed=4 * 4 * n * n + 24 * 4 * qc * n, transcendentals=0),
        compiler_params=pltpu.CompilerParams(vmem_limit_bytes=GRANT),
    )(got, pltpu.with_memory_space_constraint(panels, pltpu.HBM), old)


def body(l_rows, v_prev, l_tail, k_cross, k_query):
    x_id, y_id, k_id = lax.axis_index("x"), lax.axis_index("y"), lax.axis_index("k")
    zh_id, zl_id = lax.axis_index("zh"), lax.axis_index("zl")
    rows = l_rows.shape[0]
    qc = k_cross.shape[1]

    block = l_tail.T
    turn = [
        (((x * 4 + y) * 4 + h) * 4 + l, ((x * 4 + l) * 4 + h) * 4 + y)
        for x in range(4) for y in range(4) for h in range(4) for l in range(4) if h != x
    ]
    other = swap(block)
    turned = lax.ppermute(block, ("x", "y", "zh", "zl"), turn)
    inverted = invert(block, other)
    block = jnp.where(zh_id == x_id, jnp.where(zl_id == y_id, inverted, block), turned)
    panels = lax.all_gather(block, ("zh", "zl", "k"), axis=0)
    panels = panels.reshape(4, 4, rows, rows)

    vt = v_prev.T
    vt_other = swap(vt)
    l_other = swap(l_rows)
    v_pair = jnp.concatenate([vt, vt_other], axis=1)
    l_pair = jnp.concatenate([l_rows, l_other], axis=1)
    v_half = lax.dynamic_slice_in_dim(v_pair, k_id * qc, qc, 0)
    v_all = share(v_half, PLANE_T, 16)
    update_all = contract(v_all, l_pair, ((2,), (1,)))
    prior = contract(v_all, v_pair, ((2,), (1,)))


    both = jnp.concatenate([update_all, prior], axis=2).reshape(4, 4, qc, -1)
    both = lax.all_to_all(both, "zl", 0, 0).sum(0)
    panels, both = lax.optimization_barrier((panels, both))
    both = lax.all_to_all(both, "zh", 0, 0)
    both = both.sum(0)
    rest = k_cross.T - both[:, :rows]
    prior = both[:, rows:]

    own = lax.dynamic_slice_in_dim(panels, x_id, 1, 0)[0]
    sent = local(pack_kernel, f32(3, rows // 2, rows), own)
    got = [
        lax.ppermute(sent[: 3 - d], "y", [(y, y + 1 + d) for y in range(3 - d)]) for d in range(3)
    ]
    mine = jnp.concatenate(got, axis=0)
    theirs = swap(mine)
    inverse = local(rows_kernel, f32(4, rows, rows), own, mine, theirs, flops=8 * 12 * rows**3)

    partial_rest = rest
    right = share(rest, "y", 4)
    solved = ()
    for j in range(4):
        solved, sent = local(
            functools.partial(solve_kernel, j), (f32(qc, rows), f32(4, qc, rows)),
            right, inverse, *solved, flops=12 * 4 * qc * rows * rows,
        )
        if j < 3:
            solved = (solved,)
            got = lax.all_to_all(sent, "x", 0, 0)
            partial_rest, sent = update(j, got, panels, partial_rest)
            right = lax.all_to_all(sent, "y", 0, 0)

    near = lax.all_to_all(sent, "zh", 0, 0)
    near = share(near, "zl", 4)
    far = swap(near)
    flops = 12 * 16 * qc * qc * rows
    part = local(gram_kernel, f32(qc, 16 * qc), near, solved, flops=flops)
    part = local(split_kernel, f32(16, qc // 2, 128), part, far, solved, flops=flops)
    part = lax.all_to_all(part, PLANE_T, 0, 0)
    posterior = local(final_kernel, f32(qc, 2 * qc), part, prior, k_query.T).T
    return solved.T, posterior


def solution(mesh):
    fine = Mesh(mesh.devices.reshape(4, 4, 4, 4, 2), ("x", "y", "zh", "zl", "k"))
    row, col = ("x", "y"), ("zh", "zl", "k")
    in_specs = (P(row, col), P(col, row), P(row, col), P(row, col), P(row, col))
    return jax.shard_map(body, mesh=fine, in_specs=in_specs, out_specs=(P(row, col), P(row, col)), check_vma=False)
```

profile of v0, /device:TPU:6, one launch (start us, length us, event | category | flops | bytes accessed | tf_op | source)
XLA Modules:
  0.0 294.7 jit_solution(13002382509741204002)
XLA Ops:
  11.5 7.7 %invert_block.1 = f32[128,256]{1,0:T(8,128)S(1)} custom-call(f32[128,256]{1,0:T(8,128)S(1)} %bitcast.22, f32[128,256]{1,0:T(8,128)S(1)} %collective-permute-done.other_ref), custom_call_target="tpu_custom_call" | custom-call | flops 3221225472 | bytes 393216 | tf_op jit(solution)/shard_map/invert_block/pallas_call | solution.py:69
  24.7 12.6 %all-to-all-start = ((f32[16,32,1024]{2,1,0:T(8,128)}), f32[16,32,1024]{2,1,0:T(8,128)S(1)}, u32[]{:S(2)}, u32[]{:S(2)}) async-start(f32[16,32,1024]{2,1,0:T(8,128)} %broadcast_in_dim.6), calls=%async_computation | async-start | bytes 4194304 | tf_op jit(solution)/shard_map/all_to_all | solution.py:25
  39.2 28.0 %all-to-all-done = f32[16,32,1024]{2,1,0:T(8,128)S(1)} async-done(((f32[16,32,1024]{2,1,0:T(8,128)}), f32[16,32,1024]{2,1,0:T(8,128)S(1)}, u32[]{:S(2)}, u32[]{:S(2)}) %all-to-all-start) | async-done | bytes 2097184 | tf_op jit(solution)/shard_map/all_to_all | solution.py:25
  71.8 6.2 %all-to-all-start.1 = ((f32[4,4,32,320]{3,2,1,0:T(8,128)}), f32[4,4,32,320]{3,2,1,0:T(8,128)S(1)}, u32[]{:S(2)}, u32[]{:S(2)}) async-start(f32[4,4,32,320]{3,2,1,0:T(8,128)} %bitcast.6), calls=%async_computation.1 | async-start | bytes 1572864 | tf_op jit(solution)/shard_map/all_to_all | solution.py:213
  78.0 25.9 %all-to-all-done.1 = f32[4,4,32,320]{3,2,1,0:T(8,128)S(1)} async-done(((f32[4,4,32,320]{3,2,1,0:T(8,128)}), f32[4,4,32,320]{3,2,1,0:T(8,128)S(1)}, u32[]{:S(2)}, u32[]{:S(2)}) %all-to-all-start.1) | async-done | bytes 655392 | tf_op jit(solution)/shard_map/all_to_all | solution.py:213
  103.9 8.4 %all-gather.3.cloned.1.call-done = f32[4096,256]{1,0:T(8,128)} async-done(((f32[128,256]{1,0:T(8,128)}), f32[4096,256]{1,0:T(8,128)}) %all-gather.3.cloned.1.call-update) | async-done | bytes 4194320 | tf_op jit(solution)/shard_map/all_gather | solution.py:198
  113.6 2.8 collective-permute-start.4
  116.5 4.3 %collective-permute-start.5 = (f32[2,128,256]{2,1,0:T(8,128)S(1)}, f32[2,128,256]{2,1,0:T(8,128)S(1)}, u32[]{:S(2)}, u32[]{:S(2)}) collective-permute-start(f32[2,128,256]{2,1,0:T(8,128)S(1)} %slice.17), channel_id=1, source_target_pairs={{0,64},{32,96},{1,65},{33,97},{2,66},{34,98},{3,67},{35,99},{4,68}... | collective-permute-start | bytes 786440 | tf_op jit(solution)/shard_map/ppermute | solution.py:223
  122.1 3.8 %collective-permute-done.4 = f32[3,128,256]{2,1,0:T(8,128)S(1)} collective-permute-done((f32[3,128,256]{2,1,0:T(8,128)S(1)}, f32[3,128,256]{2,1,0:T(8,128)S(1)}, u32[]{:S(2)}, u32[]{:S(2)}) %collective-permute-start.4) | collective-permute-done | bytes 393248 | tf_op jit(solution)/shard_map/ppermute | solution.py:223
  125.9 4.9 %collective-permute-done.5 = f32[2,128,256]{2,1,0:T(8,128)S(1)} collective-permute-done((f32[2,128,256]{2,1,0:T(8,128)S(1)}, f32[2,128,256]{2,1,0:T(8,128)S(1)}, u32[]{:S(2)}, u32[]{:S(2)}) %collective-permute-start.5) | collective-permute-done | bytes 262176 | tf_op jit(solution)/shard_map/ppermute | solution.py:223
  132.8 21.5 %all_to_all.65 = f32[4,32,320]{2,1,0:T(8,128)S(1)} all-to-all(f32[4,32,320]{2,1,0:T(8,128)S(1)} %reduce_sum.18), channel_id=1, replica_groups=mesh['x'=4,'y'=4,'zh'=4,'zl'=4,'k'=2] {'zh'}, dimensions={0} | all-to-all | bytes 327680 | tf_op jit(solution)/shard_map/all_to_all | solution.py:215
  155.0 8.3 %all-to-all-start.3 = ((f32[4,32,256]{2,1,0:T(8,128)}), f32[4,32,256]{2,1,0:T(8,128)S(1)}, u32[]{:S(2)}, u32[]{:S(2)}) async-start(f32[4,32,256]{2,1,0:T(8,128)} %broadcast_in_dim.7), calls=%async_computation.3 | async-start | bytes 262144 | tf_op jit(solution)/shard_map/all_to_all | solution.py:25
  165.3 3.9 %shard_map.69.inv_ref = f32[4,256,256]{2,1,0:T(8,128)S(1)} custom-call(f32[4,256,256]{2,1,0:T(8,128)S(1)} %dynamic-slice_bitcast_fusion.own_ref, f32[6,128,256]{2,1,0:T(8,128)S(1)} %constant_dynamic-update-slice_fusion.mine_ref, f32[6,128,256]{2,1,0:T(8,128)S(1)} %copy-done.3), custom_call_target="tpu_custom_call" | custom-call | flops 1610612736 | bytes 3670016 | tf_op jit(solution)/shard_map/pallas_call | solution.py:39
  169.9 8.2 %all_to_all.66.got_ref = f32[4,32,256]{2,1,0:T(8,128)S(1)} all-to-all(f32[4,32,256]{2,1,0:T(8,128)S(1)} %get-tuple-element.19), channel_id=1, replica_groups=mesh['x'=4,'y'=4,'zh'=4,'zl'=4,'k'=2] {'x'}, dimensions={0} | all-to-all | bytes 262144 | tf_op jit(solution)/shard_map/all_to_all | solution.py:239
  180.5 12.6 %all_to_all.67.right_ref = f32[4,4,32,256]{3,2,1,0:T(8,128)S(1)} all-to-all(f32[4,4,32,256]{3,2,1,0:T(8,128)S(1)} %get-tuple-element.20), channel_id=1, replica_groups=mesh['x'=4,'y'=4,'zh'=4,'zl'=4,'k'=2] {'y'}, dimensions={0} | all-to-all | bytes 1048576 | tf_op jit(solution)/shard_map/all_to_all | solution.py:241
  193.8 8.4 %all_to_all.68.got_ref = f32[4,32,256]{2,1,0:T(8,128)S(1)} all-to-all(f32[4,32,256]{2,1,0:T(8,128)S(1)} %get-tuple-element.22), channel_id=1, replica_groups=mesh['x'=4,'y'=4,'zh'=4,'zl'=4,'k'=2] {'x'}, dimensions={0} | all-to-all | bytes 262144 | tf_op jit(solution)/shard_map/all_to_all | solution.py:239
  204.4 10.5 %all_to_all.69.right_ref = f32[4,4,32,256]{3,2,1,0:T(8,128)S(1)} all-to-all(f32[4,4,32,256]{3,2,1,0:T(8,128)S(1)} %get-tuple-element.24), channel_id=1, replica_groups=mesh['x'=4,'y'=4,'zh'=4,'zl'=4,'k'=2] {'y'}, dimensions={0} | all-to-all | bytes 1048576 | tf_op jit(solution)/shard_map/all_to_all | solution.py:241
  215.6 8.4 %all_to_all.70.got_ref = f32[4,32,256]{2,1,0:T(8,128)S(1)} all-to-all(f32[4,32,256]{2,1,0:T(8,128)S(1)} %get-tuple-element.26), channel_id=1, replica_groups=mesh['x'=4,'y'=4,'zh'=4,'zl'=4,'k'=2] {'x'}, dimensions={0} | all-to-all | bytes 262144 | tf_op jit(solution)/shard_map/all_to_all | solution.py:239
  223.9 3.0 %shard_map.75 = (f32[4,32,256]{2,1,0:T(8,128)}, f32[4,4,32,256]{3,2,1,0:T(8,128)S(1)}) custom-call(f32[4,32,256]{2,1,0:T(8,128)S(1)} %all_to_all.70.got_ref, f32[4,4,256,256]{3,2,1,0:T(8,128)} %bitcast.28, f32[4,32,256]{2,1,0:T(8,128)S(1)} %get-tuple-element.27.old_ref), custom_call_target="tpu_custom_call" | custom-call | flops 100663296 | bytes 1835008 | tf_op jit(solution)/shard_map/pallas_call | solution.py:172
  226.9 10.5 %all_to_all.71.right_ref = f32[4,4,32,256]{3,2,1,0:T(8,128)S(1)} all-to-all(f32[4,4,32,256]{3,2,1,0:T(8,128)S(1)} %get-tuple-element.28), channel_id=1, replica_groups=mesh['x'=4,'y'=4,'zh'=4,'zl'=4,'k'=2] {'y'}, dimensions={0} | all-to-all | bytes 1048576 | tf_op jit(solution)/shard_map/all_to_all | solution.py:241
  238.7 18.6 %all_to_all.72 = f32[4,32,256]{2,1,0:T(8,128)S(1)} all-to-all(f32[4,32,256]{2,1,0:T(8,128)S(1)} %get-tuple-element.31), channel_id=1, replica_groups=mesh['x'=4,'y'=4,'zh'=4,'zl'=4,'k'=2] {'zh'}, dimensions={0} | all-to-all | bytes 262144 | tf_op jit(solution)/shard_map/all_to_all | solution.py:243
  257.3 13.4 %all_to_all.73.all_ref = f32[4,4,32,256]{3,2,1,0:T(8,128)S(1)} all-to-all(f32[4,4,32,256]{3,2,1,0:T(8,128)S(1)} %broadcast_in_dim.8), channel_id=1, replica_groups=mesh['x'=4,'y'=4,'zh'=4,'zl'=4,'k'=2] {'zl'}, dimensions={0} | all-to-all | bytes 1048576 | tf_op jit(solution)/shard_map/all_to_all | solution.py:25
  275.8 5.4 %all-to-all-start.12 = ((f32[16,16,128]{2,1,0:T(8,128)}), f32[16,16,128]{2,1,0:T(8,128)S(1)}, u32[]{:S(2)}, u32[]{:S(2)}) async-start(f32[16,16,128]{2,1,0:T(8,128)} %shard_map.78), calls=%async_computation.12 | async-start | bytes 262144 | tf_op jit(solution)/shard_map/all_to_all | solution.py:249
  281.2 5.8 %all-to-all-done.12.part_ref = f32[16,16,128]{2,1,0:T(8,128)S(1)} async-done(((f32[16,16,128]{2,1,0:T(8,128)}), f32[16,16,128]{2,1,0:T(8,128)S(1)}, u32[]{:S(2)}, u32[]{:S(2)}) %all-to-all-start.12) | async-done | bytes 131104 | tf_op jit(solution)/shard_map/all_to_all | solution.py:249
  (60 shorter events, 37.6 us)
Async XLA Ops:
  7.2 105.1 %all-gather.3.cloned.1.call-start = ((), (), s32[]{:S(2)}) async-start(), calls=%async_computation.13 | async-start | bytes 4325376 | tf_op jit(solution)/shard_map/all_gather | solution.py:198
  8.2 3.2 %collective-permute-start = (f32[128,256]{1,0:T(8,128)S(1)}, f32[128,256]{1,0:T(8,128)S(1)}, u32[]{:S(2)}, u32[]{:S(2)}) collective-permute-start(f32[128,256]{1,0:T(8,128)S(1)} %bitcast.20), channel_id=1, source_target_pairs={{0,1},{1,0},{2,3},{3,2},{4,5},{5,4},{6,7},{7,6},{8,9},{9,8},{10,11... | collective-permute-start | bytes 393224 | tf_op jit(solution)/shard_map/ppermute | solution.py:29
  10.1 9.0 %collective-permute-start.1 = (f32[128,256]{1,0:T(8,128)S(1)}, f32[128,256]{1,0:T(8,128)S(1)}, u32[]{:S(2)}, u32[]{:S(2)}) collective-permute-start(f32[128,256]{1,0:T(8,128)S(1)} %bitcast.21), channel_id=1, source_target_pairs={{8,8},{10,40},{12,72},{14,104},{16,16},{18,48},{20,80},{22,112},{2... | collective-permute-start | bytes 393224 | tf_op jit(solution)/shard_map/ppermute | solution.py:195
  10.8 9.0 %copy-start.5 = (f32[512,64]{0,1:T(8,128)S(1)}, f32[512,64]{0,1:T(8,128)}, u32[]{:S(2)}) copy-start(f32[512,64]{0,1:T(8,128)} %param.6) | copy-start | bytes 393220
  19.8 3.2 %collective-permute-start.2 = (f32[64,512]{1,0:T(8,128)S(1)}, f32[64,512]{1,0:T(8,128)S(1)}, u32[]{:S(2)}, u32[]{:S(2)}) collective-permute-start(f32[64,512]{1,0:T(8,128)S(1)} %bitcast.29), channel_id=1, source_target_pairs={{0,1},{1,0},{2,3},{3,2},{4,5},{5,4},{6,7},{7,6},{8,9},{9,8},{10,11... | collective-permute-start | bytes 393224 | tf_op jit(solution)/shard_map/ppermute | solution.py:29
  24.7 12.6 %copy-start.4 = (f32[256,512]{1,0:T(8,128)S(1)}, f32[256,512]{1,0:T(8,128)}, u32[]{:S(2)}) copy-start(f32[256,512]{1,0:T(8,128)} %param.5) | copy-start | bytes 1572868
  24.7 42.5 %all-to-all-start = ((f32[16,32,1024]{2,1,0:T(8,128)}), f32[16,32,1024]{2,1,0:T(8,128)S(1)}, u32[]{:S(2)}, u32[]{:S(2)}) async-start(f32[16,32,1024]{2,1,0:T(8,128)} %broadcast_in_dim.6), calls=%async_computation | async-start | bytes 4194304 | tf_op jit(solution)/shard_map/all_to_all | solution.py:25
  37.3 31.7 %collective-permute-start.3 = (f32[256,512]{1,0:T(8,128)S(1)}, f32[256,512]{1,0:T(8,128)S(1)}, u32[]{:S(2)}, u32[]{:S(2)}) collective-permute-start(f32[256,512]{1,0:T(8,128)S(1)} %copy-done.4), channel_id=1, source_target_pairs={{0,1},{1,0},{2,3},{3,2},{4,5},{5,4},{6,7},{7,6},{8,9},{9,8},{10,11... | collective-permute-start | bytes 1572872 | tf_op jit(solution)/shard_map/ppermute | solution.py:29
  71.8 32.1 %all-to-all-start.1 = ((f32[4,4,32,320]{3,2,1,0:T(8,128)}), f32[4,4,32,320]{3,2,1,0:T(8,128)S(1)}, u32[]{:S(2)}, u32[]{:S(2)}) async-start(f32[4,4,32,320]{3,2,1,0:T(8,128)} %bitcast.6), calls=%async_computation.1 | async-start | bytes 1572864 | tf_op jit(solution)/shard_map/all_to_all | solution.py:213
  113.6 40.8 %copy-start.6 = (f32[256,32]{0,1:T(8,128)S(1)}, f32[256,32]{0,1:T(8,128)}, u32[]{:S(2)}) copy-start(f32[256,32]{0,1:T(8,128)} %param.8) | copy-start | bytes 98308
  113.6 12.3 %collective-permute-start.4 = (f32[3,128,256]{2,1,0:T(8,128)S(1)}, f32[3,128,256]{2,1,0:T(8,128)S(1)}, u32[]{:S(2)}, u32[]{:S(2)}) collective-permute-start(f32[3,128,256]{2,1,0:T(8,128)S(1)} %shard_map.68), channel_id=1, source_target_pairs={{0,32},{32,64},{64,96},{1,33},{33,65},{65,97},{2,34},{34,66},{66,9... | collective-permute-start | bytes 1179656 | tf_op jit(solution)/shard_map/ppermute | solution.py:223
  116.5 14.4 %collective-permute-start.5 = (f32[2,128,256]{2,1,0:T(8,128)S(1)}, f32[2,128,256]{2,1,0:T(8,128)S(1)}, u32[]{:S(2)}, u32[]{:S(2)}) collective-permute-start(f32[2,128,256]{2,1,0:T(8,128)S(1)} %slice.17), channel_id=1, source_target_pairs={{0,64},{32,96},{1,65},{33,97},{2,66},{34,98},{3,67},{35,99},{4,68}... | collective-permute-start | bytes 786440 | tf_op jit(solution)/shard_map/ppermute | solution.py:223
  120.8 10.1 %collective-permute-start.6 = (f32[1,128,256]{2,1,0:T(8,128)S(1)}, f32[1,128,256]{2,1,0:T(8,128)S(1)}, u32[]{:S(2)}, u32[]{:S(2)}) collective-permute-start(f32[1,128,256]{2,1,0:T(8,128)S(1)} %slice.18), channel_id=1, source_target_pairs={{0,96},{1,97},{2,98},{3,99},{4,100},{5,101},{6,102},{7,103},{8,104... | collective-permute-start | bytes 393224 | tf_op jit(solution)/shard_map/ppermute | solution.py:223
  130.9 32.4 %collective-permute-start.7 = (f32[6,128,256]{2,1,0:T(8,128)S(1)}, f32[6,128,256]{2,1,0:T(8,128)S(1)}, u32[]{:S(2)}, u32[]{:S(2)}) collective-permute-start(f32[6,128,256]{2,1,0:T(8,128)S(1)} %constant_dynamic-update-slice_fusion.mine_ref), channel_id=1, source_target_pairs={{0,1},{1,0},{2,3},{3,2},{4,5},{5,4},{6,7},{7,6},{8,9},{9,8},{10,11... | collective-permute-start | bytes 2359304 | tf_op jit(solution)/shard_map/ppermute | solution.py:29
  155.0 14.2 %all-to-all-start.3 = ((f32[4,32,256]{2,1,0:T(8,128)}), f32[4,32,256]{2,1,0:T(8,128)S(1)}, u32[]{:S(2)}, u32[]{:S(2)}) async-start(f32[4,32,256]{2,1,0:T(8,128)} %broadcast_in_dim.7), calls=%async_computation.3 | async-start | bytes 262144 | tf_op jit(solution)/shard_map/all_to_all | solution.py:25
  163.3 0.9 copy-start.2
  164.2 1.1 copy-start.3
  238.7 48.4 %copy-start.1 = (f32[64,32]{0,1:T(8,128)S(1)}, f32[64,32]{0,1:T(8,128)}, u32[]{:S(2)}) copy-start(f32[64,32]{0,1:T(8,128)} %param.9) | copy-start | bytes 24580
  270.6 3.8 %collective-permute-start.8 = (f32[4,4,32,256]{3,2,1,0:T(8,128)S(1)}, f32[4,4,32,256]{3,2,1,0:T(8,128)S(1)}, u32[]{:S(2)}, u32[]{:S(2)}) collective-permute-start(f32[4,4,32,256]{3,2,1,0:T(8,128)S(1)} %all_to_all.73.all_ref), channel_id=1, source_target_pairs={{0,1},{1,0},{2,3},{3,2},{4,5},{5,4},{6,7},{7,6},{8,9},{9,8},{10,11... | collective-permute-start | bytes 1572872 | tf_op jit(solution)/shard_map/ppermute | solution.py:29
  272.6 0.8 copy-start
  275.8 11.2 %all-to-all-start.12 = ((f32[16,16,128]{2,1,0:T(8,128)}), f32[16,16,128]{2,1,0:T(8,128)S(1)}, u32[]{:S(2)}, u32[]{:S(2)}) async-start(f32[16,16,128]{2,1,0:T(8,128)} %shard_map.78), calls=%async_computation.12 | async-start | bytes 262144 | tf_op jit(solution)/shard_map/all_to_all | solution.py:249
Sparse Core Ops, SparseCore 0:
  20.0 92.2 all-gather.2
where the time goes:
time: 298 us; the launch traced here: 295 us
  blocking collectives  112 us (38%)
  waiting for transfers between devices  79.2 us (27%)
  starting transfers between devices  51.2 us (17%)
  Pallas kernels  25.1 us (8%)
  between operations  14.4 us (5%)
  local copies, waits for them, and re-layouts  7.47 us (3%)
  matrix products  3.61 us (1%)
    all_to_all x3, blocking collectives, body(): right = lax.all_to_all(sent, 'y', 0, 0)  33.6 us
    all_to_all x2, waiting for transfers between devices, share(): lax.all_to_all(jnp.broadcast_to(value[None], (count,) + value.shape), axi...  28.1 us
    all_to_all x1, waiting for transfers between devices, body(): both = lax.all_to_all(both, 'zl', 0, 0).sum(0)  25.9 us
    all_to_all x3, blocking collectives, body(): got = lax.all_to_all(sent, 'x', 0, 0)  24.9 us
    all_to_all x1, blocking collectives, body(): both = lax.all_to_all(both, 'zh', 0, 0)  21.5 us
    all_to_all x2, starting transfers between devices, share(): lax.all_to_all(jnp.broadcast_to(value[None], (count,) + value.shape), axi...  20.8 us
    all_to_all x1, blocking collectives, body(): near = lax.all_to_all(sent, 'zh', 0, 0)  18.6 us
    all_to_all x1, blocking collectives, share(): lax.all_to_all(jnp.broadcast_to(value[None], (count,) + value.shape), axi...  13.4 us
  transfers between devices with their start and end apart: 14, of which 10 were waited for; matrix products, arithmetic and copies ran while one was open for 2% of the time, Pallas kernels for 4%

commit v1 on v0

--- a/solution.py
+++ b/solution.py
@@ -50,16 +50,21 @@
     first = lax.axis_index("k") == 0
     a, b = own_ref[...], other_ref[...]
     u = jnp.concatenate([jnp.where(first, a, b), jnp.where(first, b, a)], axis=0)
-    n = u.shape[0]
+    n = u.shape[0] // 2
     row = lax.broadcasted_iota(jnp.int32, (n, n), 0)
     col = lax.broadcasted_iota(jnp.int32, (n, n), 1)
-    x = jnp.where(row == col, 1.0 / u, 0.0)
+    us = [u[:n, :n], u[n:, n:]]
+    xs = [jnp.where(row == col, 1.0 / v, 0.0) for v in us]
     s = 0
     while (1 << s) < n:
         above = ((row >> (s + 1)) == (col >> (s + 1))) & (((row >> s) & 1) == 0) & (((col >> s) & 1) == 1)
-        x = x - mul(mul(x, jnp.where(above, u, 0.0)), x)
+        ts = [mul(x, jnp.where(above, v, 0.0)) for x, v in zip(xs, us)]
+        xs = [x - mul(t, x) for x, t in zip(xs, ts)]
         s += 1
-    full[...] = x
+    full[:n, :n] = xs[0]
+    full[n:, n:] = xs[1]
+    full[:n, n:] = -mul(mul(xs[0], u[:n, n:]), xs[1])
+    full[n:, :n] = jnp.zeros((n, n), jnp.float32)
     half = o_ref.shape[0]
     o_ref[...] = full[pl.ds(pl.multiple_of(lax.axis_index("k") * half, half), half), :]
 
@@ -76,6 +81,10 @@
         compiler_params=pltpu.CompilerParams(vmem_limit_bytes=GRANT),
         name="invert_block",
     )(own, other)
+
+
+def copy_kernel(a_ref, o_ref):
+    o_ref[...] = a_ref[...]
 
 
 def pack_kernel(own_ref, o_ref):
@@ -153,15 +162,11 @@
     o_ref[...] = query_ref[...] - (prior_ref[...] + total[:, : 2 * qc])
 
 
-def update_kernel(j, got_ref, panel_ref, old_ref, new_ref, sent_ref, held, sems):
-    copies = [pltpu.make_async_copy(panel_ref.at[j, m], held.at[m], sems.at[m]) for m in range(4)]
-    for copy in copies:
-        copy.start()
+def update_kernel(j, got_ref, panel_ref, old_ref, new_ref, sent_ref):
     known = got_ref[j]
     for m in range(4):
         old = jnp.where(lax.axis_index("y") == m, old_ref[...], 0.0) if j == 0 else old_ref[m]
-        copies[m].wait()
-        value = old - mul(known, held[m])
+        value = old - mul(known, panel_ref[0, m])
         new_ref[m] = value
         for to in range(4):
             sent_ref[to, m] = value
@@ -169,12 +174,14 @@
 
 def update(j, got, panels, old):
     qc, n = got.shape[1:]
+    whole = lambda a: pl.BlockSpec(a.shape, lambda i: (0,) * a.ndim)
+    outs = (f32(4, qc, n), f32(4, 4, qc, n))
     return pl.pallas_call(
         functools.partial(update_kernel, j),
-        out_shape=(f32(4, qc, n), f32(4, 4, qc, n)),
-        in_specs=[VMEM, pl.BlockSpec(memory_space=pltpu.HBM), VMEM],
-        out_specs=(VMEM, VMEM),
-        scratch_shapes=[pltpu.VMEM((4, n, n), jnp.float32), pltpu.SemaphoreType.DMA((4,))],
+        out_shape=outs,
+        grid=(1,),
+        in_specs=[whole(got), pl.BlockSpec((1,) + panels.shape[1:], lambda i: (j, 0, 0, 0)), whole(old)],
+        out_specs=tuple(whole(o) for o in outs),
         cost_estimate=pl.CostEstimate(flops=12 * 4 * qc * n * n, bytes_accessed=4 * 4 * n * n + 24 * 4 * qc * n, transcendentals=0),
         compiler_params=pltpu.CompilerParams(vmem_limit_bytes=GRANT),
     )(got, pltpu.with_memory_space_constraint(panels, pltpu.HBM), old)
@@ -211,10 +218,10 @@
 
     both = jnp.concatenate([update_all, prior], axis=2).reshape(4, 4, qc, -1)
     both = lax.all_to_all(both, "zl", 0, 0).sum(0)
-    panels, both = lax.optimization_barrier((panels, both))
     both = lax.all_to_all(both, "zh", 0, 0)
     both = both.sum(0)
-    rest = k_cross.T - both[:, :rows]
+    cross = local(copy_kernel, f32(qc, rows), k_cross.T)
+    rest = cross - both[:, :rows]
     prior = both[:, rows:]
 
     own = lax.dynamic_slice_in_dim(panels, x_id, 1, 0)[0]

time: 298 us -> 299 us (level)
  blocking collectives: 112 us -> 92.6 us
  waiting for transfers between devices: 79.2 us -> 94.7 us
  starting transfers between devices: 51.2 us -> 59.5 us
  Pallas kernels: 25.1 us -> 20 us
    all_to_all x1, waiting for transfers between devices: 25.9 us -> 0.01 us  [body(): both = lax.all_to_all(both, 'zl', 0, 0).sum(0)]
    all_gather x1, waiting for transfers between devices: 8.36 us -> 33.6 us  [body(): panels = lax.all_gather(block, ('zh', 'zl', 'k'), axis=0)]
    all_to_all x1 -> x0, blocking collectives: 21.5 us -> none  [body(): both = lax.all_to_all(both, 'zh', 0, 0)]
    all_to_all x0 -> x1, waiting for transfers between devices: none -> 16.4 us  [body(): both = lax.all_to_all(both, 'zh', 0, 0)]
    all_to_all x0 -> x1, starting transfers between devices: none -> 5.6 us  [body(): both = lax.all_to_all(both, 'zh', 0, 0)]
    pallas_call x1, Pallas kernels: 7.66 us -> 3.67 us  [invert(): pl.pallas_call(invert_kernel, out_shape=f32(half, n), in_specs=[VMEM, VME...]
    pallas_call x9 -> x10, Pallas kernels: 9.91 us -> 9.9 us  [local(): pl.pallas_call(kernel, out_shape=out_shape, in_specs=[VMEM] * len(operand...]
  transfers between devices with their start and end apart: 14 -> 15, of which waited for: 10 -> 10; matrix products, arithmetic and copies ran while one was open for 2% -> 3% of each run, Pallas kernels for 4% -> 3%
where the time goes in v1:
time: 299 us; the launch traced here: 296 us
  waiting for transfers between devices  94.7 us (32%)
  blocking collectives  92.6 us (31%)
  starting transfers between devices  59.5 us (20%)
  Pallas kernels  20 us (7%)
  between operations  14.4 us (5%)
  local copies, waits for them, and re-layouts  7.52 us (3%)
  matrix products  3.61 us (1%)
  other arithmetic  3.6 us (1%)
    all_gather x1, waiting for transfers between devices, body(): panels = lax.all_gather(block, ('zh', 'zl', 'k'), axis=0)  33.6 us
    all_to_all x3, blocking collectives, body(): right = lax.all_to_all(sent, 'y', 0, 0)  33.6 us
    all_to_all x2, waiting for transfers between devices, share(): lax.all_to_all(jnp.broadcast_to(value[None], (count,) + value.shape), axi...  28.1 us
    all_to_all x3, blocking collectives, body(): got = lax.all_to_all(sent, 'x', 0, 0)  26.2 us
    all_to_all x2, starting transfers between devices, share(): lax.all_to_all(jnp.broadcast_to(value[None], (count,) + value.shape), axi...  22.3 us
    all_to_all x1, blocking collectives, body(): near = lax.all_to_all(sent, 'zh', 0, 0)  18.6 us
    all_to_all x1, waiting for transfers between devices, body(): both = lax.all_to_all(both, 'zh', 0, 0)  16.4 us
    all_to_all x1, blocking collectives, share(): lax.all_to_all(jnp.broadcast_to(value[None], (count,) + value.shape), axi...  14.3 us
  transfers between devices with their start and end apart: 15, of which 10 were waited for; matrix products, arithmetic and copies ran while one was open for 3% of the time, Pallas kernels for 3%

profile of v1, /device:TPU:6, one launch (start us, length us, event | category | flops | bytes accessed | tf_op | source)
XLA Modules:
  0.0 295.9 jit_solution(14330722007585926530)
XLA Ops:
  11.5 3.7 %invert_block.1 = f32[128,256]{1,0:T(8,128)S(1)} custom-call(f32[128,256]{1,0:T(8,128)S(1)} %bitcast.21, f32[128,256]{1,0:T(8,128)S(1)} %collective-permute-done.2.other_ref), custom_call_target="tpu_custom_call" | custom-call | flops 3221225472 | bytes 393216 | tf_op jit(solution)/shard_map/invert_block/pallas_call | solution.py:74
  20.7 16.6 %all-to-all-start = ((f32[16,32,1024]{2,1,0:T(8,128)}), f32[16,32,1024]{2,1,0:T(8,128)S(1)}, u32[]{:S(2)}, u32[]{:S(2)}) async-start(f32[16,32,1024]{2,1,0:T(8,128)} %broadcast_in_dim.6), calls=%async_computation | async-start | bytes 4194304 | tf_op jit(solution)/shard_map/all_to_all | solution.py:25
  39.2 28.0 %all-to-all-done = f32[16,32,1024]{2,1,0:T(8,128)S(1)} async-done(((f32[16,32,1024]{2,1,0:T(8,128)}), f32[16,32,1024]{2,1,0:T(8,128)S(1)}, u32[]{:S(2)}, u32[]{:S(2)}) %all-to-all-start) | async-done | bytes 2097184 | tf_op jit(solution)/shard_map/all_to_all | solution.py:25
  71.8 6.2 %all-to-all-start.1 = ((f32[4,4,32,320]{3,2,1,0:T(8,128)}), f32[4,4,32,320]{3,2,1,0:T(8,128)}, u32[]{:S(2)}, u32[]{:S(2)}) async-start(f32[4,4,32,320]{3,2,1,0:T(8,128)} %bitcast.4), calls=%async_computation.1 | async-start | bytes 1572864 | tf_op jit(solution)/shard_map/all_to_all | solution.py:220
  78.0 33.6 %all-gather.3.cloned.1.call-done = f32[4096,256]{1,0:T(8,128)} async-done(((f32[128,256]{1,0:T(8,128)}), f32[4096,256]{1,0:T(8,128)}) %all-gather.3.cloned.1.call-update) | async-done | bytes 4194320 | tf_op jit(solution)/shard_map/all_gather | solution.py:205
  113.0 3.7 %collective-permute-start.4 = (f32[3,128,256]{2,1,0:T(8,128)S(1)}, f32[3,128,256]{2,1,0:T(8,128)S(1)}, u32[]{:S(2)}, u32[]{:S(2)}) collective-permute-start(f32[3,128,256]{2,1,0:T(8,128)S(1)} %shard_map.69), channel_id=1, source_target_pairs={{0,32},{32,64},{64,96},{1,33},{33,65},{65,97},{2,34},{34,66},{66,9... | collective-permute-start | bytes 1179656 | tf_op jit(solution)/shard_map/ppermute | solution.py:230
  116.8 4.5 %collective-permute-start.5 = (f32[2,128,256]{2,1,0:T(8,128)S(1)}, f32[2,128,256]{2,1,0:T(8,128)S(1)}, u32[]{:S(2)}, u32[]{:S(2)}) collective-permute-start(f32[2,128,256]{2,1,0:T(8,128)S(1)} %slice.17), channel_id=1, source_target_pairs={{0,64},{32,96},{1,65},{33,97},{2,66},{34,98},{3,67},{35,99},{4,68}... | collective-permute-start | bytes 786440 | tf_op jit(solution)/shard_map/ppermute | solution.py:230
  122.6 3.6 %collective-permute-done.4 = f32[3,128,256]{2,1,0:T(8,128)S(1)} collective-permute-done((f32[3,128,256]{2,1,0:T(8,128)S(1)}, f32[3,128,256]{2,1,0:T(8,128)S(1)}, u32[]{:S(2)}, u32[]{:S(2)}) %collective-permute-start.4) | collective-permute-done | bytes 393248 | tf_op jit(solution)/shard_map/ppermute | solution.py:230
  126.3 4.9 %collective-permute-done.5 = f32[2,128,256]{2,1,0:T(8,128)S(1)} collective-permute-done((f32[2,128,256]{2,1,0:T(8,128)S(1)}, f32[2,128,256]{2,1,0:T(8,128)S(1)}, u32[]{:S(2)}, u32[]{:S(2)}) %collective-permute-start.5) | collective-permute-done | bytes 262176 | tf_op jit(solution)/shard_map/ppermute | solution.py:230
  135.0 5.6 %all-to-all-start.2 = ((f32[4,32,320]{2,1,0:T(8,128)}), f32[4,32,320]{2,1,0:T(8,128)S(1)}, u32[]{:S(2)}, u32[]{:S(2)}) async-start(f32[4,32,320]{2,1,0:T(8,128)} %reduce_sum.18), calls=%async_computation.2 | async-start | bytes 393216 | tf_op jit(solution)/shard_map/all_to_all | solution.py:221
  140.6 16.4 %all-to-all-done.2 = f32[4,32,320]{2,1,0:T(8,128)S(1)} async-done(((f32[4,32,320]{2,1,0:T(8,128)}), f32[4,32,320]{2,1,0:T(8,128)S(1)}, u32[]{:S(2)}, u32[]{:S(2)}) %all-to-all-start.2) | async-done | bytes 163872 | tf_op jit(solution)/shard_map/all_to_all | solution.py:221
  157.7 5.8 %all-to-all-start.3 = ((f32[4,32,256]{2,1,0:T(8,128)}), f32[4,32,256]{2,1,0:T(8,128)S(1)}, u32[]{:S(2)}, u32[]{:S(2)}) async-start(f32[4,32,256]{2,1,0:T(8,128)} %broadcast_in_dim.7), calls=%async_computation.3 | async-start | bytes 262144 | tf_op jit(solution)/shard_map/all_to_all | solution.py:25
  165.5 3.9 %shard_map.70.inv_ref = f32[4,256,256]{2,1,0:T(8,128)S(1)} custom-call(f32[4,256,256]{2,1,0:T(8,128)S(1)} %dynamic-slice_bitcast_fusion.own_ref, f32[6,128,256]{2,1,0:T(8,128)S(1)} %constant_dynamic-update-slice_fusion.mine_ref, f32[6,128,256]{2,1,0:T(8,128)S(1)} %copy-done.4), custom_call_target="tpu_custom_call" | custom-call | flops 1610612736 | bytes 3670016 | tf_op jit(solution)/shard_map/pallas_call | solution.py:39
  170.2 9.4 %all_to_all.65.got_ref = f32[4,32,256]{2,1,0:T(8,128)S(1)} all-to-all(f32[4,32,256]{2,1,0:T(8,128)S(1)} %get-tuple-element.15), channel_id=1, replica_groups=mesh['x'=4,'y'=4,'zh'=4,'zl'=4,'k'=2] {'x'}, dimensions={0} | all-to-all | bytes 262144 | tf_op jit(solution)/shard_map/all_to_all | solution.py:246
  181.5 12.6 %all_to_all.66.right_ref = f32[4,4,32,256]{3,2,1,0:T(8,128)S(1)} all-to-all(f32[4,4,32,256]{3,2,1,0:T(8,128)S(1)} %get-tuple-element.16), channel_id=1, replica_groups=mesh['x'=4,'y'=4,'zh'=4,'zl'=4,'k'=2] {'y'}, dimensions={0} | all-to-all | bytes 1048576 | tf_op jit(solution)/shard_map/all_to_all | solution.py:248
  194.8 8.4 %all_to_all.67.got_ref = f32[4,32,256]{2,1,0:T(8,128)S(1)} all-to-all(f32[4,32,256]{2,1,0:T(8,128)S(1)} %get-tuple-element.18), channel_id=1, replica_groups=mesh['x'=4,'y'=4,'zh'=4,'zl'=4,'k'=2] {'x'}, dimensions={0} | all-to-all | bytes 262144 | tf_op jit(solution)/shard_map/all_to_all | solution.py:246
  205.1 10.5 %all_to_all.68.right_ref = f32[4,4,32,256]{3,2,1,0:T(8,128)S(1)} all-to-all(f32[4,4,32,256]{3,2,1,0:T(8,128)S(1)} %get-tuple-element.20), channel_id=1, replica_groups=mesh['x'=4,'y'=4,'zh'=4,'zl'=4,'k'=2] {'y'}, dimensions={0} | all-to-all | bytes 1048576 | tf_op jit(solution)/shard_map/all_to_all | solution.py:248
  216.3 8.4 %all_to_all.69.got_ref = f32[4,32,256]{2,1,0:T(8,128)S(1)} all-to-all(f32[4,32,256]{2,1,0:T(8,128)S(1)} %get-tuple-element.22), channel_id=1, replica_groups=mesh['x'=4,'y'=4,'zh'=4,'zl'=4,'k'=2] {'x'}, dimensions={0} | all-to-all | bytes 262144 | tf_op jit(solution)/shard_map/all_to_all | solution.py:246
  224.6 2.6 shard_map.76
  227.2 10.5 %all_to_all.70.right_ref = f32[4,4,32,256]{3,2,1,0:T(8,128)S(1)} all-to-all(f32[4,4,32,256]{3,2,1,0:T(8,128)S(1)} %get-tuple-element.24), channel_id=1, replica_groups=mesh['x'=4,'y'=4,'zh'=4,'zl'=4,'k'=2] {'y'}, dimensions={0} | all-to-all | bytes 1048576 | tf_op jit(solution)/shard_map/all_to_all | solution.py:248
  239.0 18.6 %all_to_all.71 = f32[4,32,256]{2,1,0:T(8,128)S(1)} all-to-all(f32[4,32,256]{2,1,0:T(8,128)S(1)} %get-tuple-element.27), channel_id=1, replica_groups=mesh['x'=4,'y'=4,'zh'=4,'zl'=4,'k'=2] {'zh'}, dimensions={0} | all-to-all | bytes 262144 | tf_op jit(solution)/shard_map/all_to_all | solution.py:250
  257.6 14.3 %all_to_all.72.all_ref = f32[4,4,32,256]{3,2,1,0:T(8,128)S(1)} all-to-all(f32[4,4,32,256]{3,2,1,0:T(8,128)S(1)} %broadcast_in_dim.8), channel_id=1, replica_groups=mesh['x'=4,'y'=4,'zh'=4,'zl'=4,'k'=2] {'zl'}, dimensions={0} | all-to-all | bytes 1048576 | tf_op jit(solution)/shard_map/all_to_all | solution.py:25
  277.1 5.4 %all-to-all-start.12 = ((f32[16,16,128]{2,1,0:T(8,128)}), f32[16,16,128]{2,1,0:T(8,128)S(1)}, u32[]{:S(2)}, u32[]{:S(2)}) async-start(f32[16,16,128]{2,1,0:T(8,128)} %shard_map.79), calls=%async_computation.12 | async-start | bytes 262144 | tf_op jit(solution)/shard_map/all_to_all | solution.py:256
  282.5 5.8 %all-to-all-done.12.part_ref = f32[16,16,128]{2,1,0:T(8,128)S(1)} async-done(((f32[16,16,128]{2,1,0:T(8,128)}), f32[16,16,128]{2,1,0:T(8,128)S(1)}, u32[]{:S(2)}, u32[]{:S(2)}) %all-to-all-start.12) | async-done | bytes 131104 | tf_op jit(solution)/shard_map/all_to_all | solution.py:256
  (62 shorter events, 38.8 us)
Async XLA Ops:
  7.2 104.5 %all-gather.3.cloned.1.call-start = ((), (), s32[]{:S(2)}) async-start(), calls=%async_computation.13 | async-start | bytes 4325376 | tf_op jit(solution)/shard_map/all_gather | solution.py:205
  8.2 3.2 %collective-permute-start.2 = (f32[128,256]{1,0:T(8,128)S(1)}, f32[128,256]{1,0:T(8,128)S(1)}, u32[]{:S(2)}, u32[]{:S(2)}) collective-permute-start(f32[128,256]{1,0:T(8,128)S(1)} %bitcast.19), channel_id=1, source_target_pairs={{0,1},{1,0},{2,3},{3,2},{4,5},{5,4},{6,7},{7,6},{8,9},{9,8},{10,11... | collective-permute-start | bytes 393224 | tf_op jit(solution)/shard_map/ppermute | solution.py:29
  10.1 5.0 %collective-permute-start.3 = (f32[128,256]{1,0:T(8,128)S(1)}, f32[128,256]{1,0:T(8,128)S(1)}, u32[]{:S(2)}, u32[]{:S(2)}) collective-permute-start(f32[128,256]{1,0:T(8,128)S(1)} %bitcast.20), channel_id=1, source_target_pairs={{8,8},{10,40},{12,72},{14,104},{16,16},{18,48},{20,80},{22,112},{2... | collective-permute-start | bytes 393224 | tf_op jit(solution)/shard_map/ppermute | solution.py:202
  10.8 5.0 %copy-start.6 = (f32[512,64]{0,1:T(8,128)S(1)}, f32[512,64]{0,1:T(8,128)}, u32[]{:S(2)}) copy-start(f32[512,64]{0,1:T(8,128)} %param.6) | copy-start | bytes 393220
  15.9 3.2 %collective-permute-start = (f32[64,512]{1,0:T(8,128)S(1)}, f32[64,512]{1,0:T(8,128)S(1)}, u32[]{:S(2)}, u32[]{:S(2)}) collective-permute-start(f32[64,512]{1,0:T(8,128)S(1)} %bitcast.29), channel_id=1, source_target_pairs={{0,1},{1,0},{2,3},{3,2},{4,5},{5,4},{6,7},{7,6},{8,9},{9,8},{10,11... | collective-permute-start | bytes 393224 | tf_op jit(solution)/shard_map/ppermute | solution.py:29
  20.7 16.6 %copy-start.5 = (f32[256,512]{1,0:T(8,128)S(1)}, f32[256,512]{1,0:T(8,128)}, u32[]{:S(2)}) copy-start(f32[256,512]{1,0:T(8,128)} %param.5) | copy-start | bytes 1572868
  20.7 46.5 %all-to-all-start = ((f32[16,32,1024]{2,1,0:T(8,128)}), f32[16,32,1024]{2,1,0:T(8,128)S(1)}, u32[]{:S(2)}, u32[]{:S(2)}) async-start(f32[16,32,1024]{2,1,0:T(8,128)} %broadcast_in_dim.6), calls=%async_computation | async-start | bytes 4194304 | tf_op jit(solution)/shard_map/all_to_all | solution.py:25
  37.3 31.7 %collective-permute-start.1 = (f32[256,512]{1,0:T(8,128)S(1)}, f32[256,512]{1,0:T(8,128)S(1)}, u32[]{:S(2)}, u32[]{:S(2)}) collective-permute-start(f32[256,512]{1,0:T(8,128)S(1)} %copy-done.5), channel_id=1, source_target_pairs={{0,1},{1,0},{2,3},{3,2},{4,5},{5,4},{6,7},{7,6},{8,9},{9,8},{10,11... | collective-permute-start | bytes 1572872 | tf_op jit(solution)/shard_map/ppermute | solution.py:29
  71.8 61.3 %all-to-all-start.1 = ((f32[4,4,32,320]{3,2,1,0:T(8,128)}), f32[4,4,32,320]{3,2,1,0:T(8,128)}, u32[]{:S(2)}, u32[]{:S(2)}) async-start(f32[4,4,32,320]{3,2,1,0:T(8,128)} %bitcast.4), calls=%async_computation.1 | async-start | bytes 1572864 | tf_op jit(solution)/shard_map/all_to_all | solution.py:220
  113.0 27.6 %copy-start.1 = (f32[256,32]{0,1:T(8,128)S(1)}, f32[256,32]{0,1:T(8,128)}, u32[]{:S(2)}) copy-start(f32[256,32]{0,1:T(8,128)} %param.8) | copy-start | bytes 98308
  113.0 13.2 %collective-permute-start.4 = (f32[3,128,256]{2,1,0:T(8,128)S(1)}, f32[3,128,256]{2,1,0:T(8,128)S(1)}, u32[]{:S(2)}, u32[]{:S(2)}) collective-permute-start(f32[3,128,256]{2,1,0:T(8,128)S(1)} %shard_map.69), channel_id=1, source_target_pairs={{0,32},{32,64},{64,96},{1,33},{33,65},{65,97},{2,34},{34,66},{66,9... | collective-permute-start | bytes 1179656 | tf_op jit(solution)/shard_map/ppermute | solution.py:230
  116.8 14.4 %collective-permute-start.5 = (f32[2,128,256]{2,1,0:T(8,128)S(1)}, f32[2,128,256]{2,1,0:T(8,128)S(1)}, u32[]{:S(2)}, u32[]{:S(2)}) collective-permute-start(f32[2,128,256]{2,1,0:T(8,128)S(1)} %slice.17), channel_id=1, source_target_pairs={{0,64},{32,96},{1,65},{33,97},{2,66},{34,98},{3,67},{35,99},{4,68}... | collective-permute-start | bytes 786440 | tf_op jit(solution)/shard_map/ppermute | solution.py:230
  121.3 9.9 %collective-permute-start.6 = (f32[1,128,256]{2,1,0:T(8,128)S(1)}, f32[1,128,256]{2,1,0:T(8,128)S(1)}, u32[]{:S(2)}, u32[]{:S(2)}) collective-permute-start(f32[1,128,256]{2,1,0:T(8,128)S(1)} %slice.18), channel_id=1, source_target_pairs={{0,96},{1,97},{2,98},{3,99},{4,100},{5,101},{6,102},{7,103},{8,104... | collective-permute-start | bytes 393224 | tf_op jit(solution)/shard_map/ppermute | solution.py:230
  131.2 32.3 %collective-permute-start.7 = (f32[6,128,256]{2,1,0:T(8,128)S(1)}, f32[6,128,256]{2,1,0:T(8,128)S(1)}, u32[]{:S(2)}, u32[]{:S(2)}) collective-permute-start(f32[6,128,256]{2,1,0:T(8,128)S(1)} %constant_dynamic-update-slice_fusion.mine_ref), channel_id=1, source_target_pairs={{0,1},{1,0},{2,3},{3,2},{4,5},{5,4},{6,7},{7,6},{8,9},{9,8},{10,11... | collective-permute-start | bytes 2359304 | tf_op jit(solution)/shard_map/ppermute | solution.py:29
  135.0 22.0 %all-to-all-start.2 = ((f32[4,32,320]{2,1,0:T(8,128)}), f32[4,32,320]{2,1,0:T(8,128)S(1)}, u32[]{:S(2)}, u32[]{:S(2)}) async-start(f32[4,32,320]{2,1,0:T(8,128)} %reduce_sum.18), calls=%async_computation.2 | async-start | bytes 393216 | tf_op jit(solution)/shard_map/all_to_all | solution.py:221
  157.7 11.8 %all-to-all-start.3 = ((f32[4,32,256]{2,1,0:T(8,128)}), f32[4,32,256]{2,1,0:T(8,128)S(1)}, u32[]{:S(2)}, u32[]{:S(2)}) async-start(f32[4,32,256]{2,1,0:T(8,128)} %broadcast_in_dim.7), calls=%async_computation.3 | async-start | bytes 262144 | tf_op jit(solution)/shard_map/all_to_all | solution.py:25
  163.5 0.9 copy-start.3
  164.4 1.1 copy-start.4
  239.0 49.3 %copy-start.2 = (f32[64,32]{0,1:T(8,128)S(1)}, f32[64,32]{0,1:T(8,128)}, u32[]{:S(2)}) copy-start(f32[64,32]{0,1:T(8,128)} %param.9) | copy-start | bytes 24580
  271.9 3.8 %collective-permute-start.8 = (f32[4,4,32,256]{3,2,1,0:T(8,128)S(1)}, f32[4,4,32,256]{3,2,1,0:T(8,128)S(1)}, u32[]{:S(2)}, u32[]{:S(2)}) collective-permute-start(f32[4,4,32,256]{3,2,1,0:T(8,128)S(1)} %all_to_all.72.all_ref), channel_id=1, source_target_pairs={{0,1},{1,0},{2,3},{3,2},{4,5},{5,4},{6,7},{7,6},{8,9},{9,8},{10,11... | collective-permute-start | bytes 1572872 | tf_op jit(solution)/shard_map/ppermute | solution.py:29
  273.8 0.8 copy-start
  277.1 11.2 %all-to-all-start.12 = ((f32[16,16,128]{2,1,0:T(8,128)}), f32[16,16,128]{2,1,0:T(8,128)S(1)}, u32[]{:S(2)}, u32[]{:S(2)}) async-start(f32[16,16,128]{2,1,0:T(8,128)} %shard_map.79), calls=%async_computation.12 | async-start | bytes 262144 | tf_op jit(solution)/shard_map/all_to_all | solution.py:256
Sparse Core Ops, SparseCore 0:
  16.0 95.6 all-gather.2

commit v2 on v1

--- a/solution.py
+++ b/solution.py
@@ -48,8 +48,7 @@
 
 def invert_kernel(own_ref, other_ref, o_ref, full):
     first = lax.axis_index("k") == 0
-    a, b = own_ref[...], other_ref[...]
-    u = jnp.concatenate([jnp.where(first, a, b), jnp.where(first, b, a)], axis=0)
+    u = joined(first, own_ref[...], other_ref[...])
     n = u.shape[0] // 2
     row = lax.broadcasted_iota(jnp.int32, (n, n), 0)
     col = lax.broadcasted_iota(jnp.int32, (n, n), 1)
@@ -87,24 +86,25 @@
     o_ref[...] = a_ref[...]
 
 
+def joined(first, mine, other):
+    return jnp.concatenate([jnp.where(first, mine, other), jnp.where(first, other, mine)], axis=0)
+
+
 def pack_kernel(own_ref, o_ref):
-    half = o_ref.shape[1]
-    rows = pl.ds(pl.multiple_of(lax.axis_index("k") * half, half), half)
     for slot, block in enumerate((lax.axis_index("y"), 0, 1)):
-        o_ref[slot] = own_ref[block, rows, :]
-
-
-def rows_kernel(own_ref, mine_ref, other_ref, o_ref):
+        o_ref[slot] = own_ref[block]
+
+
+def rows_kernel(own_ref, own_other_ref, mine_ref, other_ref, o_ref):
     y = lax.axis_index("y")
     first = lax.axis_index("k") == 0
-    n = own_ref.shape[1]
+    n = own_ref.shape[2]
 
     def block(slot):
-        a, b = mine_ref[slot], other_ref[slot]
-        return jnp.concatenate([jnp.where(first, a, b), jnp.where(first, b, a)], axis=0)
-
-    diag = own_ref[y]
-    a = mul(own_ref[:3].reshape(3 * n, n), diag)
+        return joined(first, mine_ref[slot], other_ref[slot])
+
+    diag = joined(first, own_ref[y], own_other_ref[y])
+    a = mul(jnp.concatenate([joined(first, own_ref[m], own_other_ref[m]) for m in range(3)], axis=0), diag)
     zero = jnp.zeros_like(diag)
     near, far = block(0), block(3)
     y2 = jnp.where(y > 2, -mul(near, a[2 * n :]), zero)
@@ -162,29 +162,32 @@
     o_ref[...] = query_ref[...] - (prior_ref[...] + total[:, : 2 * qc])
 
 
-def update_kernel(j, got_ref, panel_ref, old_ref, new_ref, sent_ref):
+def update_kernel(j, got_ref, panel_ref, other_ref, old_ref, new_ref, sent_ref):
+    first = lax.axis_index("k") == 0
     known = got_ref[j]
     for m in range(4):
         old = jnp.where(lax.axis_index("y") == m, old_ref[...], 0.0) if j == 0 else old_ref[m]
-        value = old - mul(known, panel_ref[0, m])
+        value = old - mul(known, joined(first, panel_ref[0, m], other_ref[0, m]))
         new_ref[m] = value
         for to in range(4):
             sent_ref[to, m] = value
 
 
-def update(j, got, panels, old):
+def update(j, got, panels, others, old):
     qc, n = got.shape[1:]
     whole = lambda a: pl.BlockSpec(a.shape, lambda i: (0,) * a.ndim)
     outs = (f32(4, qc, n), f32(4, 4, qc, n))
+    panel = pl.BlockSpec((1,) + panels.shape[1:], lambda i: (j, 0, 0, 0))
+    in_hbm = lambda a: pltpu.with_memory_space_constraint(a, pltpu.HBM)
     return pl.pallas_call(
         functools.partial(update_kernel, j),
         out_shape=outs,
         grid=(1,),
-        in_specs=[whole(got), pl.BlockSpec((1,) + panels.shape[1:], lambda i: (j, 0, 0, 0)), whole(old)],
+        in_specs=[whole(got), panel, panel, whole(old)],
         out_specs=tuple(whole(o) for o in outs),
         cost_estimate=pl.CostEstimate(flops=12 * 4 * qc * n * n, bytes_accessed=4 * 4 * n * n + 24 * 4 * qc * n, transcendentals=0),
         compiler_params=pltpu.CompilerParams(vmem_limit_bytes=GRANT),
-    )(got, pltpu.with_memory_space_constraint(panels, pltpu.HBM), old)
+    )(got, in_hbm(panels), in_hbm(others), old)
 
 
 def body(l_rows, v_prev, l_tail, k_cross, k_query):
@@ -192,6 +195,11 @@
     zh_id, zl_id = lax.axis_index("zh"), lax.axis_index("zl")
     rows = l_rows.shape[0]
     qc = k_cross.shape[1]
+
+    vt = v_prev.T
+    vt_other = swap(vt)
+    v_pair = jnp.concatenate([vt, vt_other], axis=1)
+    v_half = lax.dynamic_slice_in_dim(v_pair, k_id * qc, qc, 0)
 
     block = l_tail.T
     turn = [
@@ -202,15 +210,12 @@
     turned = lax.ppermute(block, ("x", "y", "zh", "zl"), turn)
     inverted = invert(block, other)
     block = jnp.where(zh_id == x_id, jnp.where(zl_id == y_id, inverted, block), turned)
-    panels = lax.all_gather(block, ("zh", "zl", "k"), axis=0)
-    panels = panels.reshape(4, 4, rows, rows)
-
-    vt = v_prev.T
-    vt_other = swap(vt)
+    block, v_half = lax.optimization_barrier((block, v_half))
+    panels = lax.all_gather(block, ("zh", "zl"), axis=0)
+    panels = panels.reshape(4, 4, rows // 2, rows)
+
     l_other = swap(l_rows)
-    v_pair = jnp.concatenate([vt, vt_other], axis=1)
     l_pair = jnp.concatenate([l_rows, l_other], axis=1)
-    v_half = lax.dynamic_slice_in_dim(v_pair, k_id * qc, qc, 0)
     v_all = share(v_half, PLANE_T, 16)
     update_all = contract(v_all, l_pair, ((2,), (1,)))
     prior = contract(v_all, v_pair, ((2,), (1,)))
@@ -231,7 +236,9 @@
     ]
     mine = jnp.concatenate(got, axis=0)
     theirs = swap(mine)
-    inverse = local(rows_kernel, f32(4, rows, rows), own, mine, theirs, flops=8 * 12 * rows**3)
+    others = swap(panels)
+    own_others = lax.dynamic_slice_in_dim(others, x_id, 1, 0)[0]
+    inverse = local(rows_kernel, f32(4, rows, rows), own, own_others, mine, theirs, flops=8 * 12 * rows**3)
 
     partial_rest = rest
     right = share(rest, "y", 4)
@@ -244,7 +251,7 @@
         if j < 3:
             solved = (solved,)
             got = lax.all_to_all(sent, "x", 0, 0)
-            partial_rest, sent = update(j, got, panels, partial_rest)
+            partial_rest, sent = update(j, got, panels, others, partial_rest)
             right = lax.all_to_all(sent, "y", 0, 0)
 
     near = lax.all_to_all(sent, "zh", 0, 0)

time: 299 us -> 283 us (0.946)
  waiting for transfers between devices: 94.7 us -> 82.7 us
    ppermute x3, waiting for transfers between devices: 8.5 us -> 2.75 us  [body(): lax.ppermute(sent[:3 - d], 'y', [(y, y + 1 + d) for y in range(3 - d)])]
    all_to_all x1, waiting for transfers between devices: 16.4 us -> 11 us  [body(): both = lax.all_to_all(both, 'zh', 0, 0)]
    all_to_all x2, starting transfers between devices: 22.3 us -> 18 us  [share(): lax.all_to_all(jnp.broadcast_to(value[None], (count,) + value.shape), axi...]
    ppermute x5 -> x6, starting transfers between devices: 9.73 us -> 12 us  [swap(): return lax.ppermute(value, 'k', [(0, 1), (1, 0)])]
  transfers between devices with their start and end apart: 15 -> 16, of which waited for: 10 -> 7; matrix products, arithmetic and copies ran while one was open for 3% -> 4% of each run, Pallas kernels for 3% -> 3%
where the time goes in v2:
time: 283 us; the launch traced here: 280 us
  blocking collectives  90.6 us (32%)
  waiting for transfers between devices  82.7 us (29%)
  starting transfers between devices  59.8 us (21%)
  Pallas kernels  20.1 us (7%)
  between operations  14.4 us (5%)
  local copies, waits for them, and re-layouts  6.33 us (2%)
  matrix products  3.61 us (1%)
    all_gather x1, waiting for transfers between devices, body(): panels = lax.all_gather(block, ('zh', 'zl'), axis=0)  36.4 us
    all_to_all x3, blocking collectives, body(): right = lax.all_to_all(sent, 'y', 0, 0)  32.7 us
    all_to_all x2, waiting for transfers between devices, share(): lax.all_to_all(jnp.broadcast_to(value[None], (count,) + value.shape), axi...  26.2 us
    all_to_all x3, blocking collectives, body(): got = lax.all_to_all(sent, 'x', 0, 0)  25.7 us
    all_to_all x1, blocking collectives, body(): near = lax.all_to_all(sent, 'zh', 0, 0)  19.2 us
    all_to_all x2, starting transfers between devices, share(): lax.all_to_all(jnp.broadcast_to(value[None], (count,) + value.shape), axi...  18 us
    all_to_all x1, blocking collectives, share(): lax.all_to_all(jnp.broadcast_to(value[None], (count,) + value.shape), axi...  13 us
    ppermute x6, starting transfers between devices, swap(): return lax.ppermute(value, 'k', [(0, 1), (1, 0)])  12 us
  transfers between devices with their start and end apart: 16, of which 7 were waited for; matrix products, arithmetic and copies ran while one was open for 4% of the time, Pallas kernels for 3%

profile of v2, /device:TPU:6, one launch (start us, length us, event | category | flops | bytes accessed | tf_op | source)
XLA Modules:
  0.0 280.0 jit_solution(9859809920870430999)
XLA Ops:
  10.8 2.4 collective-permute-start.2
  13.3 3.7 %invert_block.1 = f32[128,256]{1,0:T(8,128)S(1)} custom-call(f32[128,256]{1,0:T(8,128)S(1)} %bitcast.23, f32[128,256]{1,0:T(8,128)S(1)} %collective-permute-done.other_ref), custom_call_target="tpu_custom_call" | custom-call | flops 3221225472 | bytes 393216 | tf_op jit(solution)/shard_map/invert_block/pallas_call | solution.py:73
  19.3 14.7 %all-to-all-start = ((f32[16,32,1024]{2,1,0:T(8,128)}), f32[16,32,1024]{2,1,0:T(8,128)S(1)}, u32[]{:S(2)}, u32[]{:S(2)}) async-start(f32[16,32,1024]{2,1,0:T(8,128)} %broadcast_in_dim.6), calls=%async_computation | async-start | bytes 4194304 | tf_op jit(solution)/shard_map/all_to_all | solution.py:25
  35.9 25.3 %all-to-all-done = f32[16,32,1024]{2,1,0:T(8,128)S(1)} async-done(((f32[16,32,1024]{2,1,0:T(8,128)}), f32[16,32,1024]{2,1,0:T(8,128)S(1)}, u32[]{:S(2)}, u32[]{:S(2)}) %all-to-all-start) | async-done | bytes 2097184 | tf_op jit(solution)/shard_map/all_to_all | solution.py:25
  65.8 6.5 %all-to-all-start.1 = ((f32[4,4,32,320]{3,2,1,0:T(8,128)}), f32[4,4,32,320]{3,2,1,0:T(8,128)S(1)}, u32[]{:S(2)}, u32[]{:S(2)}) async-start(f32[4,4,32,320]{3,2,1,0:T(8,128)} %bitcast.5), calls=%async_computation.1 | async-start | bytes 1572864 | tf_op jit(solution)/shard_map/all_to_all | solution.py:225
  72.3 36.4 %all-gather.3.cloned.1.call-done = f32[2048,256]{1,0:T(8,128)} async-done(((f32[128,256]{1,0:T(8,128)}), f32[2048,256]{1,0:T(8,128)}) %all-gather.3.cloned.1.call-update) | async-done | bytes 2097168 | tf_op jit(solution)/shard_map/all_gather | solution.py:214
  111.8 3.2 %collective-permute-start.5 = (f32[3,128,256]{2,1,0:T(8,128)S(1)}, f32[3,128,256]{2,1,0:T(8,128)S(1)}, u32[]{:S(2)}, u32[]{:S(2)}) collective-permute-start(f32[3,128,256]{2,1,0:T(8,128)S(1)} %shard_map.69), channel_id=1, source_target_pairs={{0,32},{32,64},{64,96},{1,33},{33,65},{65,97},{2,34},{34,66},{66,9... | collective-permute-start | bytes 1179656 | tf_op jit(solution)/shard_map/ppermute | solution.py:235
  115.0 4.7 %collective-permute-start.6 = (f32[2,128,256]{2,1,0:T(8,128)S(1)}, f32[2,128,256]{2,1,0:T(8,128)S(1)}, u32[]{:S(2)}, u32[]{:S(2)}) collective-permute-start(f32[2,128,256]{2,1,0:T(8,128)S(1)} %slice.17), channel_id=1, source_target_pairs={{0,64},{32,96},{1,65},{33,97},{2,66},{34,98},{3,67},{35,99},{4,68}... | collective-permute-start | bytes 786440 | tf_op jit(solution)/shard_map/ppermute | solution.py:235
  120.5 8.0 %all-to-all-start.2 = ((f32[4,32,320]{2,1,0:T(8,128)}), f32[4,32,320]{2,1,0:T(8,128)S(1)}, u32[]{:S(2)}, u32[]{:S(2)}) async-start(f32[4,32,320]{2,1,0:T(8,128)} %reduce_sum.18), calls=%async_computation.2 | async-start | bytes 393216 | tf_op jit(solution)/shard_map/all_to_all | solution.py:226
  129.9 2.7 collective-permute-done.7
  134.6 11.0 %all-to-all-done.2 = f32[4,32,320]{2,1,0:T(8,128)S(1)} async-done(((f32[4,32,320]{2,1,0:T(8,128)}), f32[4,32,320]{2,1,0:T(8,128)S(1)}, u32[]{:S(2)}, u32[]{:S(2)}) %all-to-all-start.2) | async-done | bytes 163872 | tf_op jit(solution)/shard_map/all_to_all | solution.py:226
  146.3 3.3 %all-to-all-start.3 = ((f32[4,32,256]{2,1,0:T(8,128)}), f32[4,32,256]{2,1,0:T(8,128)S(1)}, u32[]{:S(2)}, u32[]{:S(2)}) async-start(f32[4,32,256]{2,1,0:T(8,128)} %broadcast_in_dim.7), calls=%async_computation.3 | async-start | bytes 262144 | tf_op jit(solution)/shard_map/all_to_all | solution.py:25
  150.7 3.9 %shard_map.70.inv_ref = f32[4,256,256]{2,1,0:T(8,128)S(1)} custom-call(f32[4,128,256]{2,1,0:T(8,128)S(1)} %dynamic-slice_bitcast_fusion.1.own_ref, f32[4,128,256]{2,1,0:T(8,128)S(1)} %dynamic-slice_bitcast_fusion.own_other_ref, f32[6,128,256]{2,1,0:T(8,128)S(1)} %constant_dynamic-update-slice_fusion.mine_ref, f32[6,128,256]{2,1,0:T(8,128)S(1)} %collective-permute-done.8.other_ref), custom_call_target="tpu_custom_call" | custom-call | flops 1610612736 | bytes 3670016 | tf_op jit(solution)/shard_map/pallas_call | solution.py:39
  156.2 9.0 %all_to_all.65.got_ref = f32[4,32,256]{2,1,0:T(8,128)S(1)} all-to-all(f32[4,32,256]{2,1,0:T(8,128)S(1)} %get-tuple-element.19), channel_id=1, replica_groups=mesh['x'=4,'y'=4,'zh'=4,'zl'=4,'k'=2] {'x'}, dimensions={0} | all-to-all | bytes 262144 | tf_op jit(solution)/shard_map/all_to_all | solution.py:253
  167.2 11.7 %all_to_all.66.right_ref = f32[4,4,32,256]{3,2,1,0:T(8,128)S(1)} all-to-all(f32[4,4,32,256]{3,2,1,0:T(8,128)S(1)} %get-tuple-element.20), channel_id=1, replica_groups=mesh['x'=4,'y'=4,'zh'=4,'zl'=4,'k'=2] {'y'}, dimensions={0} | all-to-all | bytes 1048576 | tf_op jit(solution)/shard_map/all_to_all | solution.py:255
  179.6 8.4 %all_to_all.67.got_ref = f32[4,32,256]{2,1,0:T(8,128)S(1)} all-to-all(f32[4,32,256]{2,1,0:T(8,128)S(1)} %get-tuple-element.22), channel_id=1, replica_groups=mesh['x'=4,'y'=4,'zh'=4,'zl'=4,'k'=2] {'x'}, dimensions={0} | all-to-all | bytes 262144 | tf_op jit(solution)/shard_map/all_to_all | solution.py:253
  189.9 10.5 %all_to_all.68.right_ref = f32[4,4,32,256]{3,2,1,0:T(8,128)S(1)} all-to-all(f32[4,4,32,256]{3,2,1,0:T(8,128)S(1)} %get-tuple-element.24), channel_id=1, replica_groups=mesh['x'=4,'y'=4,'zh'=4,'zl'=4,'k'=2] {'y'}, dimensions={0} | all-to-all | bytes 1048576 | tf_op jit(solution)/shard_map/all_to_all | solution.py:255
  201.1 8.4 %all_to_all.69.got_ref = f32[4,32,256]{2,1,0:T(8,128)S(1)} all-to-all(f32[4,32,256]{2,1,0:T(8,128)S(1)} %get-tuple-element.26), channel_id=1, replica_groups=mesh['x'=4,'y'=4,'zh'=4,'zl'=4,'k'=2] {'x'}, dimensions={0} | all-to-all | bytes 262144 | tf_op jit(solution)/shard_map/all_to_all | solution.py:253
  209.4 2.6 shard_map.76
  212.0 10.5 %all_to_all.70.right_ref = f32[4,4,32,256]{3,2,1,0:T(8,128)S(1)} all-to-all(f32[4,4,32,256]{3,2,1,0:T(8,128)S(1)} %get-tuple-element.28), channel_id=1, replica_groups=mesh['x'=4,'y'=4,'zh'=4,'zl'=4,'k'=2] {'y'}, dimensions={0} | all-to-all | bytes 1048576 | tf_op jit(solution)/shard_map/all_to_all | solution.py:255
  223.8 19.2 %all_to_all.71 = f32[4,32,256]{2,1,0:T(8,128)S(1)} all-to-all(f32[4,32,256]{2,1,0:T(8,128)S(1)} %get-tuple-element.31), channel_id=1, replica_groups=mesh['x'=4,'y'=4,'zh'=4,'zl'=4,'k'=2] {'zh'}, dimensions={0} | all-to-all | bytes 262144 | tf_op jit(solution)/shard_map/all_to_all | solution.py:257
  243.0 13.0 %all_to_all.72.all_ref = f32[4,4,32,256]{3,2,1,0:T(8,128)S(1)} all-to-all(f32[4,4,32,256]{3,2,1,0:T(8,128)S(1)} %broadcast_in_dim.8), channel_id=1, replica_groups=mesh['x'=4,'y'=4,'zh'=4,'zl'=4,'k'=2] {'zl'}, dimensions={0} | all-to-all | bytes 1048576 | tf_op jit(solution)/shard_map/all_to_all | solution.py:25
  261.2 5.4 %all-to-all-start.12 = ((f32[16,16,128]{2,1,0:T(8,128)}), f32[16,16,128]{2,1,0:T(8,128)S(1)}, u32[]{:S(2)}, u32[]{:S(2)}) async-start(f32[16,16,128]{2,1,0:T(8,128)} %shard_map.79), calls=%async_computation.12 | async-start | bytes 262144 | tf_op jit(solution)/shard_map/all_to_all | solution.py:263
  266.6 5.8 %all-to-all-done.12.part_ref = f32[16,16,128]{2,1,0:T(8,128)S(1)} async-done(((f32[16,16,128]{2,1,0:T(8,128)}), f32[16,16,128]{2,1,0:T(8,128)S(1)}, u32[]{:S(2)}, u32[]{:S(2)}) %all-to-all-start.12) | async-done | bytes 131104 | tf_op jit(solution)/shard_map/all_to_all | solution.py:263
  (61 shorter events, 35.4 us)
Async XLA Ops:
  7.2 101.5 %all-gather.3.cloned.1.call-start = ((), (), s32[]{:S(2)}) async-start(), calls=%async_computation.13 | async-start | bytes 2228224 | tf_op jit(solution)/shard_map/all_gather | solution.py:214
  8.2 5.0 %collective-permute-start = (f32[128,256]{1,0:T(8,128)S(1)}, f32[128,256]{1,0:T(8,128)S(1)}, u32[]{:S(2)}, u32[]{:S(2)}) collective-permute-start(f32[128,256]{1,0:T(8,128)S(1)} %bitcast.21), channel_id=1, source_target_pairs={{0,1},{1,0},{2,3},{3,2},{4,5},{5,4},{6,7},{7,6},{8,9},{9,8},{10,11... | collective-permute-start | bytes 393224 | tf_op jit(solution)/shard_map/ppermute | solution.py:29
  10.1 6.8 %collective-permute-start.1 = (f32[128,256]{1,0:T(8,128)S(1)}, f32[128,256]{1,0:T(8,128)S(1)}, u32[]{:S(2)}, u32[]{:S(2)}) collective-permute-start(f32[128,256]{1,0:T(8,128)S(1)} %bitcast.22), channel_id=1, source_target_pairs={{8,8},{10,40},{12,72},{14,104},{16,16},{18,48},{20,80},{22,112},{2... | collective-permute-start | bytes 393224 | tf_op jit(solution)/shard_map/ppermute | solution.py:210
  10.8 6.1 %collective-permute-start.2 = (f32[64,512]{1,0:T(8,128)}, f32[64,512]{1,0:T(8,128)S(1)}, u32[]{:S(2)}, u32[]{:S(2)}) collective-permute-start(f32[64,512]{1,0:T(8,128)} %bitcast.32), channel_id=1, source_target_pairs={{0,1},{1,0},{2,3},{3,2},{4,5},{5,4},{6,7},{7,6},{8,9},{9,8},{10,11... | collective-permute-start | bytes 393224 | tf_op jit(solution)/shard_map/ppermute | solution.py:29
  13.2 3.7 %copy-start.4 = (f32[512,64]{0,1:T(8,128)S(1)}, f32[512,64]{0,1:T(8,128)}, u32[]{:S(2)}) copy-start(f32[512,64]{0,1:T(8,128)} %param.6) | copy-start | bytes 393220
  19.3 14.7 %copy-start.3 = (f32[256,512]{1,0:T(8,128)S(1)}, f32[256,512]{1,0:T(8,128)}, u32[]{:S(2)}) copy-start(f32[256,512]{1,0:T(8,128)} %param.5) | copy-start | bytes 1572868
  19.3 41.9 %all-to-all-start = ((f32[16,32,1024]{2,1,0:T(8,128)}), f32[16,32,1024]{2,1,0:T(8,128)S(1)}, u32[]{:S(2)}, u32[]{:S(2)}) async-start(f32[16,32,1024]{2,1,0:T(8,128)} %broadcast_in_dim.6), calls=%async_computation | async-start | bytes 4194304 | tf_op jit(solution)/shard_map/all_to_all | solution.py:25
  34.0 29.0 %collective-permute-start.3 = (f32[256,512]{1,0:T(8,128)S(1)}, f32[256,512]{1,0:T(8,128)S(1)}, u32[]{:S(2)}, u32[]{:S(2)}) collective-permute-start(f32[256,512]{1,0:T(8,128)S(1)} %copy-done.3), channel_id=1, source_target_pairs={{0,1},{1,0},{2,3},{3,2},{4,5},{5,4},{6,7},{7,6},{8,9},{9,8},{10,11... | collective-permute-start | bytes 1572872 | tf_op jit(solution)/shard_map/ppermute | solution.py:29
  65.8 54.0 %all-to-all-start.1 = ((f32[4,4,32,320]{3,2,1,0:T(8,128)}), f32[4,4,32,320]{3,2,1,0:T(8,128)S(1)}, u32[]{:S(2)}, u32[]{:S(2)}) async-start(f32[4,4,32,320]{3,2,1,0:T(8,128)} %bitcast.5), calls=%async_computation.1 | async-start | bytes 1572864 | tf_op jit(solution)/shard_map/all_to_all | solution.py:225
  108.7 40.9 %collective-permute-start.4 = (f32[4,4,128,256]{3,2,1,0:T(8,128)}, f32[4,4,128,256]{3,2,1,0:T(8,128)}, u32[]{:S(2)}, u32[]{:S(2)}) collective-permute-start(f32[4,4,128,256]{3,2,1,0:T(8,128)} %bitcast.27), channel_id=1, source_target_pairs={{0,1},{1,0},{2,3},{3,2},{4,5},{5,4},{6,7},{7,6},{8,9},{9,8},{10,11... | collective-permute-start | bytes 6291464 | tf_op jit(solution)/shard_map/ppermute | solution.py:29
  111.7 22.8 %copy-start.1 = (f32[256,32]{0,1:T(8,128)S(1)}, f32[256,32]{0,1:T(8,128)}, u32[]{:S(2)}) copy-start(f32[256,32]{0,1:T(8,128)} %param.8) | copy-start | bytes 98308
  111.8 18.0 %collective-permute-start.5 = (f32[3,128,256]{2,1,0:T(8,128)S(1)}, f32[3,128,256]{2,1,0:T(8,128)S(1)}, u32[]{:S(2)}, u32[]{:S(2)}) collective-permute-start(f32[3,128,256]{2,1,0:T(8,128)S(1)} %shard_map.69), channel_id=1, source_target_pairs={{0,32},{32,64},{64,96},{1,33},{33,65},{65,97},{2,34},{34,66},{66,9... | collective-permute-start | bytes 1179656 | tf_op jit(solution)/shard_map/ppermute | solution.py:235
  115.0 14.8 %collective-permute-start.6 = (f32[2,128,256]{2,1,0:T(8,128)S(1)}, f32[2,128,256]{2,1,0:T(8,128)S(1)}, u32[]{:S(2)}, u32[]{:S(2)}) collective-permute-start(f32[2,128,256]{2,1,0:T(8,128)S(1)} %slice.17), channel_id=1, source_target_pairs={{0,64},{32,96},{1,65},{33,97},{2,66},{34,98},{3,67},{35,99},{4,68}... | collective-permute-start | bytes 786440 | tf_op jit(solution)/shard_map/ppermute | solution.py:235
  120.5 25.1 %all-to-all-start.2 = ((f32[4,32,320]{2,1,0:T(8,128)}), f32[4,32,320]{2,1,0:T(8,128)S(1)}, u32[]{:S(2)}, u32[]{:S(2)}) async-start(f32[4,32,320]{2,1,0:T(8,128)} %reduce_sum.18), calls=%async_computation.2 | async-start | bytes 393216 | tf_op jit(solution)/shard_map/all_to_all | solution.py:226
  128.5 4.1 %collective-permute-start.7 = (f32[1,128,256]{2,1,0:T(8,128)S(1)}, f32[1,128,256]{2,1,0:T(8,128)S(1)}, u32[]{:S(2)}, u32[]{:S(2)}) collective-permute-start(f32[1,128,256]{2,1,0:T(8,128)S(1)} %slice.18), channel_id=1, source_target_pairs={{0,96},{1,97},{2,98},{3,99},{4,100},{5,101},{6,102},{7,103},{8,104... | collective-permute-start | bytes 393224 | tf_op jit(solution)/shard_map/ppermute | solution.py:235
  132.6 18.1 %collective-permute-start.8 = (f32[6,128,256]{2,1,0:T(8,128)S(1)}, f32[6,128,256]{2,1,0:T(8,128)S(1)}, u32[]{:S(2)}, u32[]{:S(2)}) collective-permute-start(f32[6,128,256]{2,1,0:T(8,128)S(1)} %constant_dynamic-update-slice_fusion.mine_ref), channel_id=1, source_target_pairs={{0,1},{1,0},{2,3},{3,2},{4,5},{5,4},{6,7},{7,6},{8,9},{9,8},{10,11... | collective-permute-start | bytes 2359304 | tf_op jit(solution)/shard_map/ppermute | solution.py:29
  146.3 9.3 %all-to-all-start.3 = ((f32[4,32,256]{2,1,0:T(8,128)}), f32[4,32,256]{2,1,0:T(8,128)S(1)}, u32[]{:S(2)}, u32[]{:S(2)}) async-start(f32[4,32,256]{2,1,0:T(8,128)} %broadcast_in_dim.7), calls=%async_computation.3 | async-start | bytes 262144 | tf_op jit(solution)/shard_map/all_to_all | solution.py:25
  223.8 48.6 %copy-start.2 = (f32[64,32]{0,1:T(8,128)S(1)}, f32[64,32]{0,1:T(8,128)}, u32[]{:S(2)}) copy-start(f32[64,32]{0,1:T(8,128)} %param.9) | copy-start | bytes 24580
  256.0 3.8 %collective-permute-start.9 = (f32[4,4,32,256]{3,2,1,0:T(8,128)S(1)}, f32[4,4,32,256]{3,2,1,0:T(8,128)S(1)}, u32[]{:S(2)}, u32[]{:S(2)}) collective-permute-start(f32[4,4,32,256]{3,2,1,0:T(8,128)S(1)} %all_to_all.72.all_ref), channel_id=1, source_target_pairs={{0,1},{1,0},{2,3},{3,2},{4,5},{5,4},{6,7},{7,6},{8,9},{9,8},{10,11... | collective-permute-start | bytes 1572872 | tf_op jit(solution)/shard_map/ppermute | solution.py:29
  257.9 0.8 copy-start
  261.2 11.2 %all-to-all-start.12 = ((f32[16,16,128]{2,1,0:T(8,128)}), f32[16,16,128]{2,1,0:T(8,128)S(1)}, u32[]{:S(2)}, u32[]{:S(2)}) async-start(f32[16,16,128]{2,1,0:T(8,128)} %shard_map.79), calls=%async_computation.12 | async-start | bytes 262144 | tf_op jit(solution)/shard_map/all_to_all | solution.py:263
Sparse Core Ops, SparseCore 0:
  17.8 90.8 all-gather.2

commit v3 on v2

--- a/solution.py
+++ b/solution.py
@@ -90,6 +90,14 @@
     return jnp.concatenate([jnp.where(first, mine, other), jnp.where(first, other, mine)], axis=0)
 
 
+def join_kernel(*refs):
+    at = 0
+    for ref in refs[:-1]:
+        for slot in range(ref.shape[0]):
+            refs[-1][at] = ref[slot]
+            at += 1
+
+
 def pack_kernel(own_ref, o_ref):
     for slot, block in enumerate((lax.axis_index("y"), 0, 1)):
         o_ref[slot] = own_ref[block]
@@ -221,20 +229,20 @@
     prior = contract(v_all, v_pair, ((2,), (1,)))
 
 
-    both = jnp.concatenate([update_all, prior], axis=2).reshape(4, 4, qc, -1)
-    both = lax.all_to_all(both, "zl", 0, 0).sum(0)
+    prior = lax.psum_scatter(prior.reshape(16 * qc, -1), ("zl", "zh"), scatter_dimension=0, tiled=True)
+    both = lax.all_to_all(update_all.reshape(4, 4, qc, rows), "zl", 0, 0)
+    both = both.sum(0)
     both = lax.all_to_all(both, "zh", 0, 0)
     both = both.sum(0)
     cross = local(copy_kernel, f32(qc, rows), k_cross.T)
-    rest = cross - both[:, :rows]
-    prior = both[:, rows:]
+    rest = cross - both
 
     own = lax.dynamic_slice_in_dim(panels, x_id, 1, 0)[0]
     sent = local(pack_kernel, f32(3, rows // 2, rows), own)
-    got = [
-        lax.ppermute(sent[: 3 - d], "y", [(y, y + 1 + d) for y in range(3 - d)]) for d in range(3)
-    ]
-    mine = jnp.concatenate(got, axis=0)
+    got = []
+    for d in range(3):
+        got.append(lax.ppermute(sent[: 3 - d], "y", [(y, y + 1 + d) for y in range(3 - d)]))
+    mine = local(join_kernel, f32(6, rows // 2, rows), *got)
     theirs = swap(mine)
     others = swap(panels)
     own_others = lax.dynamic_slice_in_dim(others, x_id, 1, 0)[0]

time: 283 us -> 370 us (1.31)
  waiting for transfers between devices: 82.7 us -> 171 us
    reduce_scatter x0 -> x1, waiting for transfers between devices: none -> 79 us  [body(): lax.psum_scatter(prior.reshape(16 * qc, -1), ('zl', 'zh'), scatter_dimens...]
    all_gather x1, waiting for transfers between devices: 36.4 us -> 66 us  [body(): panels = lax.all_gather(block, ('zh', 'zl'), axis=0)]
    all_to_all x2, waiting for transfers between devices: 26.2 us -> 0.97 us  [share(): lax.all_to_all(jnp.broadcast_to(value[None], (count,) + value.shape), axi...]
    ppermute x3, waiting for transfers between devices: 2.75 us -> 8.61 us  [body(): lax.ppermute(sent[:3 - d], 'y', [(y, y + 1 + d) for y in range(3 - d)])]
    all_to_all x1, waiting for transfers between devices: 5.82 us -> 0.01 us  [body(): part = lax.all_to_all(part, PLANE_T, 0, 0)]
    all_to_all x1, waiting for transfers between devices: 11 us -> 16.2 us  [body(): both = lax.all_to_all(both, 'zh', 0, 0)]
    pallas_call x10 -> x11, Pallas kernels: 9.91 us -> 9.96 us  [local(): pl.pallas_call(kernel, out_shape=out_shape, in_specs=[VMEM] * len(operand...]
  transfers between devices with their start and end apart: 16 -> 17, of which waited for: 7 -> 6; matrix products, arithmetic and copies ran while one was open for 4% -> 3% of each run, Pallas kernels for 3% -> 3%
where the time goes in v3:
time: 370 us; the launch traced here: 368 us
  waiting for transfers between devices  171 us (46%)
  blocking collectives  89.9 us (24%)
  starting transfers between devices  59.1 us (16%)
  Pallas kernels  20.2 us (5%)
  between operations  14.4 us (4%)
  local copies, waits for them, and re-layouts  6.3 us (2%)
  matrix products  5.1 us (1%)
    reduce_scatter x1, waiting for transfers between devices, body(): lax.psum_scatter(prior.reshape(16 * qc, -1), ('zl', 'zh'), scatter_dimens...  79 us
    all_gather x1, waiting for transfers between devices, body(): panels = lax.all_gather(block, ('zh', 'zl'), axis=0)  66 us
    all_to_all x3, blocking collectives, body(): right = lax.all_to_all(sent, 'y', 0, 0)  32.8 us
    all_to_all x3, blocking collectives, body(): got = lax.all_to_all(sent, 'x', 0, 0)  25.4 us
    all_to_all x2, starting transfers between devices, share(): lax.all_to_all(jnp.broadcast_to(value[None], (count,) + value.shape), axi...  20 us
    all_to_all x1, blocking collectives, body(): near = lax.all_to_all(sent, 'zh', 0, 0)  18.3 us
    all_to_all x1, waiting for transfers between devices, body(): both = lax.all_to_all(both, 'zh', 0, 0)  16.2 us
    all_to_all x1, blocking collectives, share(): lax.all_to_all(jnp.broadcast_to(value[None], (count,) + value.shape), axi...  13.4 us
  transfers between devices with their start and end apart: 17, of which 6 were waited for; matrix products, arithmetic and copies ran while one was open for 3% of the time, Pallas kernels for 3%

profile of v3, /device:TPU:6, one launch (start us, length us, event | category | flops | bytes accessed | tf_op | source)
XLA Modules:
  0.0 368.3 jit_solution(1545054731338388268)
XLA Ops:
  13.3 3.7 invert_block.1
  19.4 14.7 %all-to-all-start = ((f32[16,32,1024]{2,1,0:T(8,128)}), f32[16,32,1024]{2,1,0:T(8,128)S(1)}, u32[]{:S(2)}, u32[]{:S(2)}) async-start(f32[16,32,1024]{2,1,0:T(8,128)} %broadcast_in_dim.6), calls=%async_computation | async-start | bytes 4194304 | tf_op jit(solution)/shard_map/all_to_all | solution.py:25
  36.0 66.0 %all-gather.3.cloned.1.call-done = f32[2048,256]{1,0:T(8,128)} async-done(((f32[128,256]{1,0:T(8,128)}), f32[2048,256]{1,0:T(8,128)}) %all-gather.3.cloned.1.call-update) | async-done | bytes 2097168 | tf_op jit(solution)/shard_map/all_gather | solution.py:222
  104.0 2.6 fusion
  106.6 4.1 %all-to-all-start.1 = ((f32[4,4,32,256]{3,2,1,0:T(8,128)}), f32[4,4,32,256]{3,2,1,0:T(8,128)}, u32[]{:S(2)}, u32[]{:S(2)}) async-start(f32[4,4,32,256]{3,2,1,0:T(8,128)} %bitcast.4), calls=%async_computation.1 | async-start | bytes 1048576 | tf_op jit(solution)/shard_map/all_to_all | solution.py:233
  111.9 3.4 collective-permute-start.5
  115.3 4.6 %collective-permute-start.6 = (f32[2,128,256]{2,1,0:T(8,128)S(1)}, f32[2,128,256]{2,1,0:T(8,128)S(1)}, u32[]{:S(2)}, u32[]{:S(2)}) collective-permute-start(f32[2,128,256]{2,1,0:T(8,128)S(1)} %slice.8), channel_id=1, source_target_pairs={{0,64},{32,96},{1,65},{33,97},{2,66},{34,98},{3,67},{35,99},{4,68}... | collective-permute-start | bytes 786440 | tf_op jit(solution)/shard_map/ppermute | solution.py:244
  121.3 5.9 %collective-permute-done.7.refs_2_ = f32[1,128,256]{2,1,0:T(8,128)S(1)} collective-permute-done((f32[1,128,256]{2,1,0:T(8,128)S(1)}, f32[1,128,256]{2,1,0:T(8,128)S(1)}, u32[]{:S(2)}, u32[]{:S(2)}) %collective-permute-start.7) | collective-permute-done | bytes 131104 | tf_op jit(solution)/shard_map/ppermute | solution.py:244
  127.2 2.7 collective-permute-done.6.refs_1_
  133.7 7.4 %all-to-all-start.2 = ((f32[4,32,256]{2,1,0:T(8,128)}), f32[4,32,256]{2,1,0:T(8,128)S(1)}, u32[]{:S(2)}, u32[]{:S(2)}) async-start(f32[4,32,256]{2,1,0:T(8,128)} %reduce_sum.18), calls=%async_computation.2 | async-start | bytes 262144 | tf_op jit(solution)/shard_map/all_to_all | solution.py:235
  141.0 16.2 %all-to-all-done.2 = f32[4,32,256]{2,1,0:T(8,128)S(1)} async-done(((f32[4,32,256]{2,1,0:T(8,128)}), f32[4,32,256]{2,1,0:T(8,128)S(1)}, u32[]{:S(2)}, u32[]{:S(2)}) %all-to-all-start.2) | async-done | bytes 131104 | tf_op jit(solution)/shard_map/all_to_all | solution.py:235
  157.9 5.3 %all-to-all-start.3 = ((f32[4,32,256]{2,1,0:T(8,128)}), f32[4,32,256]{2,1,0:T(8,128)S(1)}, u32[]{:S(2)}, u32[]{:S(2)}) async-start(f32[4,32,256]{2,1,0:T(8,128)} %broadcast_in_dim.7), calls=%async_computation.3 | async-start | bytes 262144 | tf_op jit(solution)/shard_map/all_to_all | solution.py:25
  164.3 3.9 %shard_map.71.inv_ref = f32[4,256,256]{2,1,0:T(8,128)S(1)} custom-call(f32[4,128,256]{2,1,0:T(8,128)S(1)} %dynamic-slice_bitcast_fusion.1.own_ref, f32[4,128,256]{2,1,0:T(8,128)S(1)} %dynamic-slice_bitcast_fusion.own_other_ref, f32[6,128,256]{2,1,0:T(8,128)S(1)} %shard_map.70.mine_ref, f32[6,128,256]{2,1,0:T(8,128)S(1)} %collective-permute-done.8.other_ref), custom_call_target="tpu_custom_call" | custom-call | flops 1610612736 | bytes 3670016 | tf_op jit(solution)/shard_map/pallas_call | solution.py:39
  169.9 8.6 %all_to_all.65.got_ref = f32[4,32,256]{2,1,0:T(8,128)S(1)} all-to-all(f32[4,32,256]{2,1,0:T(8,128)S(1)} %get-tuple-element.19), channel_id=1, replica_groups=mesh['x'=4,'y'=4,'zh'=4,'zl'=4,'k'=2] {'x'}, dimensions={0} | all-to-all | bytes 262144 | tf_op jit(solution)/shard_map/all_to_all | solution.py:261
  180.5 11.7 %all_to_all.66.right_ref = f32[4,4,32,256]{3,2,1,0:T(8,128)S(1)} all-to-all(f32[4,4,32,256]{3,2,1,0:T(8,128)S(1)} %get-tuple-element.20), channel_id=1, replica_groups=mesh['x'=4,'y'=4,'zh'=4,'zl'=4,'k'=2] {'y'}, dimensions={0} | all-to-all | bytes 1048576 | tf_op jit(solution)/shard_map/all_to_all | solution.py:263
  192.9 8.4 %all_to_all.67.got_ref = f32[4,32,256]{2,1,0:T(8,128)S(1)} all-to-all(f32[4,32,256]{2,1,0:T(8,128)S(1)} %get-tuple-element.22), channel_id=1, replica_groups=mesh['x'=4,'y'=4,'zh'=4,'zl'=4,'k'=2] {'x'}, dimensions={0} | all-to-all | bytes 262144 | tf_op jit(solution)/shard_map/all_to_all | solution.py:261
  203.2 10.5 %all_to_all.68.right_ref = f32[4,4,32,256]{3,2,1,0:T(8,128)S(1)} all-to-all(f32[4,4,32,256]{3,2,1,0:T(8,128)S(1)} %get-tuple-element.24), channel_id=1, replica_groups=mesh['x'=4,'y'=4,'zh'=4,'zl'=4,'k'=2] {'y'}, dimensions={0} | all-to-all | bytes 1048576 | tf_op jit(solution)/shard_map/all_to_all | solution.py:263
  214.3 8.4 %all_to_all.69.got_ref = f32[4,32,256]{2,1,0:T(8,128)S(1)} all-to-all(f32[4,32,256]{2,1,0:T(8,128)S(1)} %get-tuple-element.26), channel_id=1, replica_groups=mesh['x'=4,'y'=4,'zh'=4,'zl'=4,'k'=2] {'x'}, dimensions={0} | all-to-all | bytes 262144 | tf_op jit(solution)/shard_map/all_to_all | solution.py:261
  222.7 2.6 shard_map.77
  225.3 10.6 %all_to_all.70.right_ref = f32[4,4,32,256]{3,2,1,0:T(8,128)S(1)} all-to-all(f32[4,4,32,256]{3,2,1,0:T(8,128)S(1)} %get-tuple-element.28), channel_id=1, replica_groups=mesh['x'=4,'y'=4,'zh'=4,'zl'=4,'k'=2] {'y'}, dimensions={0} | all-to-all | bytes 1048576 | tf_op jit(solution)/shard_map/all_to_all | solution.py:263
  237.2 18.3 %all_to_all.71 = f32[4,32,256]{2,1,0:T(8,128)S(1)} all-to-all(f32[4,32,256]{2,1,0:T(8,128)S(1)} %get-tuple-element.31), channel_id=1, replica_groups=mesh['x'=4,'y'=4,'zh'=4,'zl'=4,'k'=2] {'zh'}, dimensions={0} | all-to-all | bytes 262144 | tf_op jit(solution)/shard_map/all_to_all | solution.py:265
  255.6 13.4 %all_to_all.72.all_ref = f32[4,4,32,256]{3,2,1,0:T(8,128)S(1)} all-to-all(f32[4,4,32,256]{3,2,1,0:T(8,128)S(1)} %broadcast_in_dim.8), channel_id=1, replica_groups=mesh['x'=4,'y'=4,'zh'=4,'zl'=4,'k'=2] {'zl'}, dimensions={0} | all-to-all | bytes 1048576 | tf_op jit(solution)/shard_map/all_to_all | solution.py:25
  275.5 5.4 %all-to-all-start.12 = ((f32[16,16,128]{2,1,0:T(8,128)}), f32[16,16,128]{2,1,0:T(8,128)S(1)}, u32[]{:S(2)}, u32[]{:S(2)}) async-start(f32[16,16,128]{2,1,0:T(8,128)} %shard_map.80), calls=%async_computation.12 | async-start | bytes 262144 | tf_op jit(solution)/shard_map/all_to_all | solution.py:271
  280.9 79.0 %reduce-scatter.2.cloned.1.call-done.prior_ref = f32[32,64]{1,0:T(8,128)} async-done(((f32[512,64]{1,0:T(8,128)}), f32[32,64]{1,0:T(8,128)}) %reduce-scatter.2.cloned.1.call-update) | async-done | bytes 8208 | tf_op jit(solution)/shard_map/reduce_scatter | solution.py:232
  (70 shorter events, 36.4 us)
Async XLA Ops:
  7.2 94.8 %all-gather.3.cloned.1.call-start = ((), (), s32[]{:S(2)}) async-start(), calls=%async_computation.15 | async-start | bytes 2228224 | tf_op jit(solution)/shard_map/all_gather | solution.py:222
  8.2 5.0 %collective-permute-start = (f32[128,256]{1,0:T(8,128)S(1)}, f32[128,256]{1,0:T(8,128)S(1)}, u32[]{:S(2)}, u32[]{:S(2)}) collective-permute-start(f32[128,256]{1,0:T(8,128)S(1)} %bitcast.22), channel_id=1, source_target_pairs={{0,1},{1,0},{2,3},{3,2},{4,5},{5,4},{6,7},{7,6},{8,9},{9,8},{10,11... | collective-permute-start | bytes 393224 | tf_op jit(solution)/shard_map/ppermute | solution.py:29
  10.1 6.9 %collective-permute-start.1 = (f32[128,256]{1,0:T(8,128)S(1)}, f32[128,256]{1,0:T(8,128)S(1)}, u32[]{:S(2)}, u32[]{:S(2)}) collective-permute-start(f32[128,256]{1,0:T(8,128)S(1)} %bitcast.23), channel_id=1, source_target_pairs={{8,8},{10,40},{12,72},{14,104},{16,16},{18,48},{20,80},{22,112},{2... | collective-permute-start | bytes 393224 | tf_op jit(solution)/shard_map/ppermute | solution.py:218
  10.8 6.1 %collective-permute-start.2 = (f32[64,512]{1,0:T(8,128)}, f32[64,512]{1,0:T(8,128)S(1)}, u32[]{:S(2)}, u32[]{:S(2)}) collective-permute-start(f32[64,512]{1,0:T(8,128)} %bitcast.34), channel_id=1, source_target_pairs={{0,1},{1,0},{2,3},{3,2},{4,5},{5,4},{6,7},{7,6},{8,9},{9,8},{10,11... | collective-permute-start | bytes 393224 | tf_op jit(solution)/shard_map/ppermute | solution.py:29
  13.2 3.7 %copy-start.7 = (f32[512,64]{0,1:T(8,128)S(1)}, f32[512,64]{0,1:T(8,128)}, u32[]{:S(2)}) copy-start(f32[512,64]{0,1:T(8,128)} %param.6) | copy-start | bytes 393220
  19.4 14.7 %copy-start.6 = (f32[256,512]{1,0:T(8,128)S(1)}, f32[256,512]{1,0:T(8,128)}, u32[]{:S(2)}) copy-start(f32[256,512]{1,0:T(8,128)} %param.5) | copy-start | bytes 1572868
  19.4 84.6 %all-to-all-start = ((f32[16,32,1024]{2,1,0:T(8,128)}), f32[16,32,1024]{2,1,0:T(8,128)S(1)}, u32[]{:S(2)}, u32[]{:S(2)}) async-start(f32[16,32,1024]{2,1,0:T(8,128)} %broadcast_in_dim.6), calls=%async_computation | async-start | bytes 4194304 | tf_op jit(solution)/shard_map/all_to_all | solution.py:25
  34.1 69.9 %collective-permute-start.3 = (f32[256,512]{1,0:T(8,128)S(1)}, f32[256,512]{1,0:T(8,128)S(1)}, u32[]{:S(2)}, u32[]{:S(2)}) collective-permute-start(f32[256,512]{1,0:T(8,128)S(1)} %copy-done.6), channel_id=1, source_target_pairs={{0,1},{1,0},{2,3},{3,2},{4,5},{5,4},{6,7},{7,6},{8,9},{9,8},{10,11... | collective-permute-start | bytes 1572872 | tf_op jit(solution)/shard_map/ppermute | solution.py:29
  102.0 61.2 %collective-permute-start.4 = (f32[4,4,128,256]{3,2,1,0:T(8,128)}, f32[4,4,128,256]{3,2,1,0:T(8,128)}, u32[]{:S(2)}, u32[]{:S(2)}) collective-permute-start(f32[4,4,128,256]{3,2,1,0:T(8,128)} %bitcast.28), channel_id=1, source_target_pairs={{0,1},{1,0},{2,3},{3,2},{4,5},{5,4},{6,7},{7,6},{8,9},{9,8},{10,11... | collective-permute-start | bytes 6291464 | tf_op jit(solution)/shard_map/ppermute | solution.py:29
  106.6 25.3 %all-to-all-start.1 = ((f32[4,4,32,256]{3,2,1,0:T(8,128)}), f32[4,4,32,256]{3,2,1,0:T(8,128)}, u32[]{:S(2)}, u32[]{:S(2)}) async-start(f32[4,4,32,256]{3,2,1,0:T(8,128)} %bitcast.4), calls=%async_computation.1 | async-start | bytes 1048576 | tf_op jit(solution)/shard_map/all_to_all | solution.py:233
  111.8 29.2 %copy-start.1 = (f32[256,32]{0,1:T(8,128)S(1)}, f32[256,32]{0,1:T(8,128)}, u32[]{:S(2)}) copy-start(f32[256,32]{0,1:T(8,128)} %param.8) | copy-start | bytes 98308
  111.9 18.0 %collective-permute-start.5 = (f32[3,128,256]{2,1,0:T(8,128)S(1)}, f32[3,128,256]{2,1,0:T(8,128)S(1)}, u32[]{:S(2)}, u32[]{:S(2)}) collective-permute-start(f32[3,128,256]{2,1,0:T(8,128)S(1)} %shard_map.69), channel_id=1, source_target_pairs={{0,32},{32,64},{64,96},{1,33},{33,65},{65,97},{2,34},{34,66},{66,9... | collective-permute-start | bytes 1179656 | tf_op jit(solution)/shard_map/ppermute | solution.py:244
  115.3 14.6 %collective-permute-start.6 = (f32[2,128,256]{2,1,0:T(8,128)S(1)}, f32[2,128,256]{2,1,0:T(8,128)S(1)}, u32[]{:S(2)}, u32[]{:S(2)}) collective-permute-start(f32[2,128,256]{2,1,0:T(8,128)S(1)} %slice.8), channel_id=1, source_target_pairs={{0,64},{32,96},{1,65},{33,97},{2,66},{34,98},{3,67},{35,99},{4,68}... | collective-permute-start | bytes 786440 | tf_op jit(solution)/shard_map/ppermute | solution.py:244
  120.0 7.2 %collective-permute-start.7 = (f32[1,128,256]{2,1,0:T(8,128)S(1)}, f32[1,128,256]{2,1,0:T(8,128)S(1)}, u32[]{:S(2)}, u32[]{:S(2)}) collective-permute-start(f32[1,128,256]{2,1,0:T(8,128)S(1)} %slice.9), channel_id=1, source_target_pairs={{0,96},{1,97},{2,98},{3,99},{4,100},{5,101},{6,102},{7,103},{8,104... | collective-permute-start | bytes 393224 | tf_op jit(solution)/shard_map/ppermute | solution.py:244
  130.0 34.4 %collective-permute-start.8 = (f32[6,128,256]{2,1,0:T(8,128)S(1)}, f32[6,128,256]{2,1,0:T(8,128)S(1)}, u32[]{:S(2)}, u32[]{:S(2)}) collective-permute-start(f32[6,128,256]{2,1,0:T(8,128)S(1)} %shard_map.70.mine_ref), channel_id=1, source_target_pairs={{0,1},{1,0},{2,3},{3,2},{4,5},{5,4},{6,7},{7,6},{8,9},{9,8},{10,11... | collective-permute-start | bytes 2359304 | tf_op jit(solution)/shard_map/ppermute | solution.py:29
  133.7 23.6 %all-to-all-start.2 = ((f32[4,32,256]{2,1,0:T(8,128)}), f32[4,32,256]{2,1,0:T(8,128)S(1)}, u32[]{:S(2)}, u32[]{:S(2)}) async-start(f32[4,32,256]{2,1,0:T(8,128)} %reduce_sum.18), calls=%async_computation.2 | async-start | bytes 262144 | tf_op jit(solution)/shard_map/all_to_all | solution.py:235
  157.9 11.3 %all-to-all-start.3 = ((f32[4,32,256]{2,1,0:T(8,128)}), f32[4,32,256]{2,1,0:T(8,128)S(1)}, u32[]{:S(2)}, u32[]{:S(2)}) async-start(f32[4,32,256]{2,1,0:T(8,128)} %broadcast_in_dim.7), calls=%async_computation.3 | async-start | bytes 262144 | tf_op jit(solution)/shard_map/all_to_all | solution.py:25
  163.2 196.7 %reduce-scatter.2.cloned.1.call-start = ((), (), s32[]{:S(2)}) async-start(), calls=%async_computation.14 | async-start | bytes 278528 | tf_op jit(solution)/shard_map/reduce_scatter | solution.py:232
  225.3 45.7 %copy-start.5 = (f32[16,32,1024]{2,1,0:T(8,128)S(1)}, f32[16,32,1024]{2,1,0:T(8,128)}, u32[]{:S(2)}) copy-start(f32[16,32,1024]{2,1,0:T(8,128)} %copy-done.4) | copy-start | bytes 6291460
  225.3 45.7 %copy-start.9 = (f32[64,512]{1,0:T(8,128)S(1)}, f32[64,512]{1,0:T(8,128)}, u32[]{:S(2)}) copy-start(f32[64,512]{1,0:T(8,128)} %copy-done.8) | copy-start | bytes 393220
  255.6 18.0 %copy-start = (f32[32,256]{1,0:T(8,128)S(1)}, f32[32,256]{1,0:T(8,128)}, u32[]{:S(2)}) copy-start(f32[32,256]{1,0:T(8,128)} %get-tuple-element.30.own_ref) | copy-start | bytes 98308
  269.0 90.9 %copy-start.2 = (f32[64,32]{0,1:T(8,128)S(1)}, f32[64,32]{0,1:T(8,128)}, u32[]{:S(2)}) copy-start(f32[64,32]{0,1:T(8,128)} %param.9) | copy-start | bytes 24580
  269.0 5.1 %collective-permute-start.9 = (f32[4,4,32,256]{3,2,1,0:T(8,128)S(1)}, f32[4,4,32,256]{3,2,1,0:T(8,128)S(1)}, u32[]{:S(2)}, u32[]{:S(2)}) collective-permute-start(f32[4,4,32,256]{3,2,1,0:T(8,128)S(1)} %all_to_all.72.all_ref), channel_id=1, source_target_pairs={{0,1},{1,0},{2,3},{3,2},{4,5},{5,4},{6,7},{7,6},{8,9},{9,8},{10,11... | collective-permute-start | bytes 1572872 | tf_op jit(solution)/shard_map/ppermute | solution.py:29
  275.5 84.4 %all-to-all-start.12 = ((f32[16,16,128]{2,1,0:T(8,128)}), f32[16,16,128]{2,1,0:T(8,128)S(1)}, u32[]{:S(2)}, u32[]{:S(2)}) async-start(f32[16,16,128]{2,1,0:T(8,128)} %shard_map.80), calls=%async_computation.12 | async-start | bytes 262144 | tf_op jit(solution)/shard_map/all_to_all | solution.py:271
  (3 other events, 5.8 us)
Sparse Core Ops, SparseCore 0:
  17.8 84.1 all-gather.2
  273.7 86.2 reduce-scatter.1

commit v4 on v3

--- a/solution.py
+++ b/solution.py
@@ -125,16 +125,18 @@
 
 
 def solve_kernel(j, right_ref, inv_ref, *refs):
-    new_ref, sent_ref = refs[-2:]
-    value = jnp.zeros(new_ref.shape, jnp.float32)
+    outs = refs[-3:] if j == 3 else refs[-2:]
+    value = jnp.zeros(outs[0].shape, jnp.float32)
     for m in range(4):
         right = right_ref[m] if j == 0 else sum(right_ref[s, m] for s in range(4))
         value = value + mul(right, inv_ref[m])
     if j > 0:
         value = jnp.where(lax.axis_index("x") == j, value, refs[0][...])
-    new_ref[...] = value
+    outs[0][...] = value
     for to in range(4):
-        sent_ref[to] = value
+        outs[1][to] = value
+    if j == 3:
+        outs[2][...] = value
 
 
 def gram_kernel(all_ref, own_ref, o_ref):
@@ -172,7 +174,7 @@
 
 def update_kernel(j, got_ref, panel_ref, other_ref, old_ref, new_ref, sent_ref):
     first = lax.axis_index("k") == 0
-    known = got_ref[j]
+    known = got_ref[j if got_ref.shape[0] > 1 else 0]
     for m in range(4):
         old = jnp.where(lax.axis_index("y") == m, old_ref[...], 0.0) if j == 0 else old_ref[m]
         value = old - mul(known, joined(first, panel_ref[0, m], other_ref[0, m]))
@@ -252,22 +254,26 @@
     right = share(rest, "y", 4)
     solved = ()
     for j in range(4):
-        solved, sent = local(
-            functools.partial(solve_kernel, j), (f32(qc, rows), f32(4, qc, rows)),
+        solved, sent, *again = local(
+            functools.partial(solve_kernel, j), (f32(qc, rows), f32(4, qc, rows)) + (f32(qc, rows),) * (j == 3),
             right, inverse, *solved, flops=12 * 4 * qc * rows * rows,
         )
         if j < 3:
             solved = (solved,)
-            got = lax.all_to_all(sent, "x", 0, 0)
+            if j == 2:
+                got = lax.ppermute(solved[0], "x", [(2, 3)])[None]
+            else:
+                got = lax.all_to_all(sent, "x", 0, 0)
             partial_rest, sent = update(j, got, panels, others, partial_rest)
             right = lax.all_to_all(sent, "y", 0, 0)
 
     near = lax.all_to_all(sent, "zh", 0, 0)
+    near, prior = lax.optimization_barrier((near, prior))
     near = share(near, "zl", 4)
     far = swap(near)
     flops = 12 * 16 * qc * qc * rows
-    part = local(gram_kernel, f32(qc, 16 * qc), near, solved, flops=flops)
-    part = local(split_kernel, f32(16, qc // 2, 128), part, far, solved, flops=flops)
+    part = local(gram_kernel, f32(qc, 16 * qc), near, again[0], flops=flops)
+    part = local(split_kernel, f32(16, qc // 2, 128), part, far, again[0], flops=flops)
     part = lax.all_to_all(part, PLANE_T, 0, 0)
     posterior = local(final_kernel, f32(qc, 2 * qc), part, prior, k_query.T).T
     return solved.T, posterior

time: 370 us -> 382 us (1.032)
  waiting for transfers between devices: 171 us -> 193 us
  blocking collectives: 89.9 us -> 78.4 us
    reduce_scatter x1, waiting for transfers between devices: 79 us -> 95.7 us  [body(): lax.psum_scatter(prior.reshape(16 * qc, -1), ('zl', 'zh'), scatter_dimens...]
    all_to_all x3 -> x2, blocking collectives: 25.4 us -> 17 us  [body(): got = lax.all_to_all(sent, 'x', 0, 0)]
    all_to_all x1, blocking collectives: 18.3 us -> 13.3 us  [body(): part = lax.all_to_all(part, PLANE_T, 0, 0)]
    ppermute x0 -> x1, waiting for transfers between devices: none -> 4.51 us  [body(): got = lax.ppermute(solved[0], 'x', [(2, 3)])[None]]
  transfers between devices with their start and end apart: 17 -> 18, of which waited for: 6 -> 8; matrix products, arithmetic and copies ran while one was open for 3% -> 3% of each run, Pallas kernels for 3% -> 2%
where the time goes in v4:
time: 382 us; the launch traced here: 379 us
  waiting for transfers between devices  193 us (51%)
  blocking collectives  78.4 us (21%)
  starting transfers between devices  58.3 us (15%)
  Pallas kernels  20.2 us (5%)
  between operations  14.4 us (4%)
  matrix products  6.7 us (2%)
  local copies, waits for them, and re-layouts  5.54 us (1%)
    reduce_scatter x1, waiting for transfers between devices, body(): lax.psum_scatter(prior.reshape(16 * qc, -1), ('zl', 'zh'), scatter_dimens...  95.7 us
    all_gather x1, waiting for transfers between devices, body(): panels = lax.all_gather(block, ('zh', 'zl'), axis=0)  66 us
    all_to_all x3, blocking collectives, body(): right = lax.all_to_all(sent, 'y', 0, 0)  32.8 us
    all_to_all x2, starting transfers between devices, share(): lax.all_to_all(jnp.broadcast_to(value[None], (count,) + value.shape), axi...  20 us
    all_to_all x2, blocking collectives, body(): got = lax.all_to_all(sent, 'x', 0, 0)  17 us
    all_to_all x1, waiting for transfers between devices, body(): both = lax.all_to_all(both, 'zh', 0, 0)  16.2 us
    all_to_all x1, blocking collectives, share(): lax.all_to_all(jnp.broadcast_to(value[None], (count,) + value.shape), axi...  15.3 us
    all_to_all x1, blocking collectives, body(): part = lax.all_to_all(part, PLANE_T, 0, 0)  13.3 us
  transfers between devices with their start and end apart: 18, of which 8 were waited for; matrix products, arithmetic and copies ran while one was open for 3% of the time, Pallas kernels for 2%

profile of v4, /device:TPU:6, one launch (start us, length us, event | category | flops | bytes accessed | tf_op | source)
XLA Modules:
  0.0 379.3 jit_solution(6504336018843355881)
XLA Ops:
  13.3 3.7 invert_block.1
  19.3 14.7 %all-to-all-start = ((f32[16,32,1024]{2,1,0:T(8,128)}), f32[16,32,1024]{2,1,0:T(8,128)S(1)}, u32[]{:S(2)}, u32[]{:S(2)}) async-start(f32[16,32,1024]{2,1,0:T(8,128)} %broadcast_in_dim.8), calls=%async_computation | async-start | bytes 4194304 | tf_op jit(solution)/shard_map/all_to_all | solution.py:25
  36.0 66.0 %all-gather.3.cloned.1.call-done = f32[2048,256]{1,0:T(8,128)} async-done(((f32[128,256]{1,0:T(8,128)}), f32[2048,256]{1,0:T(8,128)}) %all-gather.3.cloned.1.call-update) | async-done | bytes 2097168 | tf_op jit(solution)/shard_map/all_gather | solution.py:224
  104.0 2.6 fusion
  106.6 4.1 %all-to-all-start.1 = ((f32[4,4,32,256]{3,2,1,0:T(8,128)}), f32[4,4,32,256]{3,2,1,0:T(8,128)}, u32[]{:S(2)}, u32[]{:S(2)}) async-start(f32[4,4,32,256]{3,2,1,0:T(8,128)} %bitcast.4), calls=%async_computation.1 | async-start | bytes 1048576 | tf_op jit(solution)/shard_map/all_to_all | solution.py:235
  111.9 3.4 collective-permute-start.5
  115.3 4.7 %collective-permute-start.6 = (f32[2,128,256]{2,1,0:T(8,128)S(1)}, f32[2,128,256]{2,1,0:T(8,128)S(1)}, u32[]{:S(2)}, u32[]{:S(2)}) collective-permute-start(f32[2,128,256]{2,1,0:T(8,128)S(1)} %slice.8), channel_id=1, source_target_pairs={{0,64},{32,96},{1,65},{33,97},{2,66},{34,98},{3,67},{35,99},{4,68}... | collective-permute-start | bytes 786440 | tf_op jit(solution)/shard_map/ppermute | solution.py:246
  121.3 5.9 %collective-permute-done.7.refs_2_ = f32[1,128,256]{2,1,0:T(8,128)S(1)} collective-permute-done((f32[1,128,256]{2,1,0:T(8,128)S(1)}, f32[1,128,256]{2,1,0:T(8,128)S(1)}, u32[]{:S(2)}, u32[]{:S(2)}) %collective-permute-start.7) | collective-permute-done | bytes 131104 | tf_op jit(solution)/shard_map/ppermute | solution.py:246
  127.2 2.7 collective-permute-done.6.refs_1_
  133.6 7.4 %all-to-all-start.2 = ((f32[4,32,256]{2,1,0:T(8,128)}), f32[4,32,256]{2,1,0:T(8,128)S(1)}, u32[]{:S(2)}, u32[]{:S(2)}) async-start(f32[4,32,256]{2,1,0:T(8,128)} %reduce_sum.18), calls=%async_computation.2 | async-start | bytes 262144 | tf_op jit(solution)/shard_map/all_to_all | solution.py:237
  141.0 16.2 %all-to-all-done.2 = f32[4,32,256]{2,1,0:T(8,128)S(1)} async-done(((f32[4,32,256]{2,1,0:T(8,128)}), f32[4,32,256]{2,1,0:T(8,128)S(1)}, u32[]{:S(2)}, u32[]{:S(2)}) %all-to-all-start.2) | async-done | bytes 131104 | tf_op jit(solution)/shard_map/all_to_all | solution.py:237
  157.9 5.3 %all-to-all-start.3 = ((f32[4,32,256]{2,1,0:T(8,128)}), f32[4,32,256]{2,1,0:T(8,128)S(1)}, u32[]{:S(2)}, u32[]{:S(2)}) async-start(f32[4,32,256]{2,1,0:T(8,128)} %broadcast_in_dim.9), calls=%async_computation.3 | async-start | bytes 262144 | tf_op jit(solution)/shard_map/all_to_all | solution.py:25
  164.3 3.9 %shard_map.71.inv_ref = f32[4,256,256]{2,1,0:T(8,128)S(1)} custom-call(f32[4,128,256]{2,1,0:T(8,128)S(1)} %dynamic-slice_bitcast_fusion.1.own_ref, f32[4,128,256]{2,1,0:T(8,128)S(1)} %dynamic-slice_bitcast_fusion.own_other_ref, f32[6,128,256]{2,1,0:T(8,128)S(1)} %shard_map.70.mine_ref, f32[6,128,256]{2,1,0:T(8,128)S(1)} %collective-permute-done.8.other_ref), custom_call_target="tpu_custom_call" | custom-call | flops 1610612736 | bytes 3670016 | tf_op jit(solution)/shard_map/pallas_call | solution.py:39
  169.9 8.6 %all_to_all.60.got_ref = f32[4,32,256]{2,1,0:T(8,128)S(1)} all-to-all(f32[4,32,256]{2,1,0:T(8,128)S(1)} %get-tuple-element.21), channel_id=1, replica_groups=mesh['x'=4,'y'=4,'zh'=4,'zl'=4,'k'=2] {'x'}, dimensions={0} | all-to-all | bytes 262144 | tf_op jit(solution)/shard_map/all_to_all | solution.py:266
  180.4 11.7 %all_to_all.61.right_ref = f32[4,4,32,256]{3,2,1,0:T(8,128)S(1)} all-to-all(f32[4,4,32,256]{3,2,1,0:T(8,128)S(1)} %get-tuple-element.22), channel_id=1, replica_groups=mesh['x'=4,'y'=4,'zh'=4,'zl'=4,'k'=2] {'y'}, dimensions={0} | all-to-all | bytes 1048576 | tf_op jit(solution)/shard_map/all_to_all | solution.py:268
  192.8 8.4 %all_to_all.62.got_ref = f32[4,32,256]{2,1,0:T(8,128)S(1)} all-to-all(f32[4,32,256]{2,1,0:T(8,128)S(1)} %get-tuple-element.24), channel_id=1, replica_groups=mesh['x'=4,'y'=4,'zh'=4,'zl'=4,'k'=2] {'x'}, dimensions={0} | all-to-all | bytes 262144 | tf_op jit(solution)/shard_map/all_to_all | solution.py:266
  203.2 10.5 %all_to_all.63.right_ref = f32[4,4,32,256]{3,2,1,0:T(8,128)S(1)} all-to-all(f32[4,4,32,256]{3,2,1,0:T(8,128)S(1)} %get-tuple-element.26), channel_id=1, replica_groups=mesh['x'=4,'y'=4,'zh'=4,'zl'=4,'k'=2] {'y'}, dimensions={0} | all-to-all | bytes 1048576 | tf_op jit(solution)/shard_map/all_to_all | solution.py:268
  216.2 4.5 %collective-permute-done.9 = f32[32,256]{1,0:T(8,128)S(1)} collective-permute-done((f32[32,256]{1,0:T(8,128)S(1)}, f32[32,256]{1,0:T(8,128)S(1)}, u32[]{:S(2)}, u32[]{:S(2)}) %collective-permute-start.9) | collective-permute-done | bytes 32800 | tf_op jit(solution)/shard_map/ppermute | solution.py:264
  223.4 10.6 %all_to_all.64.right_ref = f32[4,4,32,256]{3,2,1,0:T(8,128)S(1)} all-to-all(f32[4,4,32,256]{3,2,1,0:T(8,128)S(1)} %get-tuple-element.30), channel_id=1, replica_groups=mesh['x'=4,'y'=4,'zh'=4,'zl'=4,'k'=2] {'y'}, dimensions={0} | all-to-all | bytes 1048576 | tf_op jit(solution)/shard_map/all_to_all | solution.py:268
  235.3 3.3 all-to-all-start.9
  238.7 4.1 %fusion.4 = f32[16,32,64]{2,1,0:T(8,128)} fusion(f32[16,32,1024]{2,1,0:T(8,128)} %copy-done.3, f32[64,512]{1,0:T(8,128)S(1)} %copy-done.7, f32[64,512]{1,0:T(8,128)S(1)} %bitcast.37), kind=kOutput, calls=%fused_computation.10 | convolution fusion | flops 402718720 | bytes 2490368 | tf_op jit(solution)/shard_map/dot_general | solution.py:17
  242.8 95.7 %reduce-scatter.2.cloned.1.call-done.prior_ref = f32[32,64]{1,0:T(8,128)} async-done(((f32[512,64]{1,0:T(8,128)}), f32[32,64]{1,0:T(8,128)}) %reduce-scatter.2.cloned.1.call-update) | async-done | bytes 8208 | tf_op jit(solution)/shard_map/reduce_scatter | solution.py:234
  338.5 15.3 %all_to_all.65.all_ref = f32[4,4,32,256]{3,2,1,0:T(8,128)S(1)} all-to-all(f32[4,4,32,256]{3,2,1,0:T(8,128)S(1)} %broadcast_in_dim.11), channel_id=1, replica_groups=mesh['x'=4,'y'=4,'zh'=4,'zl'=4,'k'=2] {'zl'}, dimensions={0} | all-to-all | bytes 1048576 | tf_op jit(solution)/shard_map/all_to_all | solution.py:25
  358.4 13.3 %all_to_all.66.part_ref = f32[16,16,128]{2,1,0:T(8,128)S(1)} all-to-all(f32[16,16,128]{2,1,0:T(8,128)S(1)} %shard_map.80), channel_id=1, replica_groups=mesh['x'=4,'y'=4,'zh'=4,'zl'=4,'k'=2] {'y','x'}, dimensions={0} | all-to-all | bytes 262144 | tf_op jit(solution)/shard_map/all_to_all | solution.py:277
  (67 shorter events, 38.3 us)
Async XLA Ops:
  7.2 94.8 %all-gather.3.cloned.1.call-start = ((), (), s32[]{:S(2)}) async-start(), calls=%async_computation.14 | async-start | bytes 2228224 | tf_op jit(solution)/shard_map/all_gather | solution.py:224
  8.2 5.0 %collective-permute-start = (f32[128,256]{1,0:T(8,128)S(1)}, f32[128,256]{1,0:T(8,128)S(1)}, u32[]{:S(2)}, u32[]{:S(2)}) collective-permute-start(f32[128,256]{1,0:T(8,128)S(1)} %bitcast.23), channel_id=1, source_target_pairs={{0,1},{1,0},{2,3},{3,2},{4,5},{5,4},{6,7},{7,6},{8,9},{9,8},{10,11... | collective-permute-start | bytes 393224 | tf_op jit(solution)/shard_map/ppermute | solution.py:29
  10.1 6.9 %collective-permute-start.1 = (f32[128,256]{1,0:T(8,128)S(1)}, f32[128,256]{1,0:T(8,128)S(1)}, u32[]{:S(2)}, u32[]{:S(2)}) collective-permute-start(f32[128,256]{1,0:T(8,128)S(1)} %bitcast.24), channel_id=1, source_target_pairs={{8,8},{10,40},{12,72},{14,104},{16,16},{18,48},{20,80},{22,112},{2... | collective-permute-start | bytes 393224 | tf_op jit(solution)/shard_map/ppermute | solution.py:220
  10.8 6.1 %collective-permute-start.2 = (f32[64,512]{1,0:T(8,128)}, f32[64,512]{1,0:T(8,128)S(1)}, u32[]{:S(2)}, u32[]{:S(2)}) collective-permute-start(f32[64,512]{1,0:T(8,128)} %bitcast.35), channel_id=1, source_target_pairs={{0,1},{1,0},{2,3},{3,2},{4,5},{5,4},{6,7},{7,6},{8,9},{9,8},{10,11... | collective-permute-start | bytes 393224 | tf_op jit(solution)/shard_map/ppermute | solution.py:29
  13.2 3.7 copy-start.5
  19.3 14.7 %copy-start.4 = (f32[256,512]{1,0:T(8,128)S(1)}, f32[256,512]{1,0:T(8,128)}, u32[]{:S(2)}) copy-start(f32[256,512]{1,0:T(8,128)} %param.5) | copy-start | bytes 1572868
  19.3 84.6 %all-to-all-start = ((f32[16,32,1024]{2,1,0:T(8,128)}), f32[16,32,1024]{2,1,0:T(8,128)S(1)}, u32[]{:S(2)}, u32[]{:S(2)}) async-start(f32[16,32,1024]{2,1,0:T(8,128)} %broadcast_in_dim.8), calls=%async_computation | async-start | bytes 4194304 | tf_op jit(solution)/shard_map/all_to_all | solution.py:25
  34.0 69.9 %collective-permute-start.3 = (f32[256,512]{1,0:T(8,128)S(1)}, f32[256,512]{1,0:T(8,128)S(1)}, u32[]{:S(2)}, u32[]{:S(2)}) collective-permute-start(f32[256,512]{1,0:T(8,128)S(1)} %copy-done.4), channel_id=1, source_target_pairs={{0,1},{1,0},{2,3},{3,2},{4,5},{5,4},{6,7},{7,6},{8,9},{9,8},{10,11... | collective-permute-start | bytes 1572872 | tf_op jit(solution)/shard_map/ppermute | solution.py:29
  102.0 61.2 %collective-permute-start.4 = (f32[4,4,128,256]{3,2,1,0:T(8,128)}, f32[4,4,128,256]{3,2,1,0:T(8,128)}, u32[]{:S(2)}, u32[]{:S(2)}) collective-permute-start(f32[4,4,128,256]{3,2,1,0:T(8,128)} %bitcast.29), channel_id=1, source_target_pairs={{0,1},{1,0},{2,3},{3,2},{4,5},{5,4},{6,7},{7,6},{8,9},{9,8},{10,11... | collective-permute-start | bytes 6291464 | tf_op jit(solution)/shard_map/ppermute | solution.py:29
  106.6 25.3 %all-to-all-start.1 = ((f32[4,4,32,256]{3,2,1,0:T(8,128)}), f32[4,4,32,256]{3,2,1,0:T(8,128)}, u32[]{:S(2)}, u32[]{:S(2)}) async-start(f32[4,4,32,256]{3,2,1,0:T(8,128)} %bitcast.4), calls=%async_computation.1 | async-start | bytes 1048576 | tf_op jit(solution)/shard_map/all_to_all | solution.py:235
  111.8 29.2 %copy-start = (f32[256,32]{0,1:T(8,128)S(1)}, f32[256,32]{0,1:T(8,128)}, u32[]{:S(2)}) copy-start(f32[256,32]{0,1:T(8,128)} %param.8) | copy-start | bytes 98308
  111.9 18.0 %collective-permute-start.5 = (f32[3,128,256]{2,1,0:T(8,128)S(1)}, f32[3,128,256]{2,1,0:T(8,128)S(1)}, u32[]{:S(2)}, u32[]{:S(2)}) collective-permute-start(f32[3,128,256]{2,1,0:T(8,128)S(1)} %shard_map.69), channel_id=1, source_target_pairs={{0,32},{32,64},{64,96},{1,33},{33,65},{65,97},{2,34},{34,66},{66,9... | collective-permute-start | bytes 1179656 | tf_op jit(solution)/shard_map/ppermute | solution.py:246
  115.3 14.6 %collective-permute-start.6 = (f32[2,128,256]{2,1,0:T(8,128)S(1)}, f32[2,128,256]{2,1,0:T(8,128)S(1)}, u32[]{:S(2)}, u32[]{:S(2)}) collective-permute-start(f32[2,128,256]{2,1,0:T(8,128)S(1)} %slice.8), channel_id=1, source_target_pairs={{0,64},{32,96},{1,65},{33,97},{2,66},{34,98},{3,67},{35,99},{4,68}... | collective-permute-start | bytes 786440 | tf_op jit(solution)/shard_map/ppermute | solution.py:246
  120.0 7.2 %collective-permute-start.7 = (f32[1,128,256]{2,1,0:T(8,128)S(1)}, f32[1,128,256]{2,1,0:T(8,128)S(1)}, u32[]{:S(2)}, u32[]{:S(2)}) collective-permute-start(f32[1,128,256]{2,1,0:T(8,128)S(1)} %slice.9), channel_id=1, source_target_pairs={{0,96},{1,97},{2,98},{3,99},{4,100},{5,101},{6,102},{7,103},{8,104... | collective-permute-start | bytes 393224 | tf_op jit(solution)/shard_map/ppermute | solution.py:246
  129.9 34.3 %collective-permute-start.8 = (f32[6,128,256]{2,1,0:T(8,128)S(1)}, f32[6,128,256]{2,1,0:T(8,128)S(1)}, u32[]{:S(2)}, u32[]{:S(2)}) collective-permute-start(f32[6,128,256]{2,1,0:T(8,128)S(1)} %shard_map.70.mine_ref), channel_id=1, source_target_pairs={{0,1},{1,0},{2,3},{3,2},{4,5},{5,4},{6,7},{7,6},{8,9},{9,8},{10,11... | collective-permute-start | bytes 2359304 | tf_op jit(solution)/shard_map/ppermute | solution.py:29
  133.6 23.6 %all-to-all-start.2 = ((f32[4,32,256]{2,1,0:T(8,128)}), f32[4,32,256]{2,1,0:T(8,128)S(1)}, u32[]{:S(2)}, u32[]{:S(2)}) async-start(f32[4,32,256]{2,1,0:T(8,128)} %reduce_sum.18), calls=%async_computation.2 | async-start | bytes 262144 | tf_op jit(solution)/shard_map/all_to_all | solution.py:237
  157.9 11.3 %all-to-all-start.3 = ((f32[4,32,256]{2,1,0:T(8,128)}), f32[4,32,256]{2,1,0:T(8,128)S(1)}, u32[]{:S(2)}, u32[]{:S(2)}) async-start(f32[4,32,256]{2,1,0:T(8,128)} %broadcast_in_dim.9), calls=%async_computation.3 | async-start | bytes 262144 | tf_op jit(solution)/shard_map/all_to_all | solution.py:25
  215.0 5.8 %collective-permute-start.9 = (f32[32,256]{1,0:T(8,128)S(1)}, f32[32,256]{1,0:T(8,128)S(1)}, u32[]{:S(2)}, u32[]{:S(2)}) collective-permute-start(f32[32,256]{1,0:T(8,128)S(1)} %get-tuple-element.28.refs_0_), channel_id=1, source_target_pairs={{256,384},{257,385},{258,386},{259,387},{260,388},{261,389},{262,3... | collective-permute-start | bytes 98312 | tf_op jit(solution)/shard_map/ppermute | solution.py:264
  223.4 15.3 %copy-start.7 = (f32[64,512]{1,0:T(8,128)S(1)}, f32[64,512]{1,0:T(8,128)}, u32[]{:S(2)}) copy-start(f32[64,512]{1,0:T(8,128)} %copy-done.6) | copy-start | bytes 393220
  235.3 103.2 %all-to-all-start.9 = ((f32[4,32,256]{2,1,0:T(8,128)}), f32[4,32,256]{2,1,0:T(8,128)S(1)}, u32[]{:S(2)}, u32[]{:S(2)}) async-start(f32[4,32,256]{2,1,0:T(8,128)} %get-tuple-element.32), calls=%async_computation.9 | async-start | bytes 262144 | tf_op jit(solution)/shard_map/all_to_all | solution.py:270
  238.6 99.8 %reduce-scatter.2.cloned.1.call-start = ((), (), s32[]{:S(2)}) async-start(), calls=%async_computation.13 | async-start | bytes 278528 | tf_op jit(solution)/shard_map/reduce_scatter | solution.py:234
  242.8 128.9 %copy-start.1 = (f32[64,32]{0,1:T(8,128)S(1)}, f32[64,32]{0,1:T(8,128)}, u32[]{:S(2)}) copy-start(f32[64,32]{0,1:T(8,128)} %param.9) | copy-start | bytes 24580
  338.5 33.2 %copy-start.2 = (f32[32,64]{1,0:T(8,128)S(1)}, f32[32,64]{1,0:T(8,128)}, u32[]{:S(2)}) copy-start(f32[32,64]{1,0:T(8,128)} %reduce-scatter.2.cloned.1.call-done.prior_ref) | copy-start | bytes 24580
  353.9 3.8 collective-permute-start.10
  (2 other events, 5.0 us)
Sparse Core Ops, SparseCore 0:
  17.8 84.1 all-gather.2
  242.9 95.5 reduce-scatter.1
